TPU v7x, 32 devices: a whole 2x2x4 slice. The times are simulated.
32 devices in a mesh: group: 2 (over x), row: 16 (over z, y, core).
Axes of the slice: x: 2, y: 2, z: 4, core: 2. Of those that a mesh axis runs over, the one named last changes fastest.
Arguments:
- pair_rep: float32 [256, 128, 128], P(('group', 'row')), parts along dimension 0, may hold values from -7 to 7
- token_mask: int32 [256], P('group'), parts along dimension 0, may hold values 0 or 1
- ln_gain: float32 [2, 128], replicated, may hold values from 0.5 to 1.5
- w_proj: bfloat16 [2, 128, 512], replicated, may hold values from -0.5 to 0.5
- w_tri: bfloat16 [2, 128, 4], replicated, may hold values from -3 to 3
- gate_bias: float32 [2, 128], replicated, may hold values from -6 to 6
- w_out: bfloat16 [2, 128, 128], replicated, may hold values from -0.5 to 0.5
- out_bias: float32 [2, 128], replicated, may hold values from -3 to 3
Outputs:
- pair_next: float32 [256, 128, 128], P('group', 'row'), parts along dimension 0
There are 2 independent parts, one for each index of `group`. A program takes and returns all parts, laid end to end along the dimension named above; an argument that names none is the same for every part. Nothing has to cross between parts.
All inputs are finite; a program needn't handle non-finite values.
Results may differ from a plain program's by a relative error of at most 0.009.
Values may be sent and summed in bfloat16 or wider, within the bound.
No kernel may reach another device: no remote copies, remote signals or barrier semaphores. Data moves between devices by JAX's collectives and lax.ppermute only.
A program may use at most 128 MiB of HBM per device.

v0:
```python
import jax
import jax.numpy as jnp
from jax import lax
from jax.sharding import PartitionSpec as P


def normed(pair_rep, gain):
    centre = jnp.mean(pair_rep, axis=-1, keepdims=True)
    shifted = pair_rep - centre
    spread = jnp.mean(shifted * shifted, axis=-1, keepdims=True)
    return (shifted * lax.rsqrt(spread + 1e-05) * gain).astype(jnp.bfloat16)


def tri_bias(normal_x, w_tri):
    return jnp.einsum("rlc,ch->hrl", normal_x, w_tri, preferred_element_type=jnp.float32).astype(
        jnp.bfloat16
    )


def make_block(normal_x, keep_mask, w_proj, w_tri, gate_bias, w_out, out_bias):
    head_count = w_tri.shape[1]
    inner_width = w_proj.shape[1] // 4
    head_dim = inner_width // head_count
    scaling = head_dim ** (-0.5)
    local_rows = normal_x.shape[0]
    key_count = normal_x.shape[1]
    projected = jnp.dot(normal_x, w_proj, preferred_element_type=jnp.float32)
    queries = (projected[..., :inner_width] * scaling).astype(jnp.bfloat16)
    key_rows = projected[..., inner_width : 2 * inner_width].astype(jnp.bfloat16)
    key_rows = key_rows.reshape(local_rows, key_count, head_count, head_dim)
    values = projected[..., 2 * inner_width : 3 * inner_width].astype(jnp.bfloat16)
    values = values.reshape(local_rows, key_count, head_count, head_dim)
    gate_act = jax.nn.sigmoid(projected[..., 3 * inner_width :] + gate_bias)

    def block(bias_part, offset):
        block_len = bias_part.shape[1]
        query_part = queries
        query_part = query_part.reshape(local_rows, block_len, head_count, head_dim)
        scores = jnp.einsum(
            "ijhd,ikhd->ihjk", query_part, key_rows, preferred_element_type=jnp.float32
        )
        scores = scores + bias_part.astype(jnp.float32)[None]
        scores = jnp.where(keep_mask[:, None, None, :], scores, jnp.float32(-1000000000.0))
        row_max = jnp.max(scores, axis=3, keepdims=True)
        weights = jnp.exp(scores - row_max)
        probabilities = (weights / jnp.sum(weights, axis=3, keepdims=True)).astype(jnp.bfloat16)
        mixture = jnp.einsum(
            "ihjk,ikhd->ijhd", probabilities, values, preferred_element_type=jnp.float32
        )
        mixture = mixture.reshape(local_rows, block_len, inner_width)
        joined = (gate_act * mixture).astype(jnp.bfloat16)
        return (
            jnp.einsum("ijc,cd->ijd", joined, w_out, preferred_element_type=jnp.float32) + out_bias
        )

    return block


def local(pair_rep, token_mask, ln_gain, w_proj, w_tri, gate_bias, w_out, out_bias):
    local_rows = pair_rep.shape[0]
    row_offset = lax.axis_index("row") * local_rows
    mask_local = lax.dynamic_slice_in_dim(token_mask, row_offset, local_rows, 0)
    keep_mask = mask_local[:, None] * token_mask[None, :] > 0
    x_start = normed(pair_rep, ln_gain[0])
    first_block = make_block(
        x_start, keep_mask, w_proj[0], w_tri[0], gate_bias[0], w_out[0], out_bias[0]
    )
    update = first_block(
        lax.all_gather(tri_bias(x_start, w_tri[0]), "row", axis=1, tiled=True), jnp.int32(0)
    )
    stacked = pair_rep + update
    bias_rows = tri_bias(normed(stacked, ln_gain[1]), w_tri[1])
    gathered = lax.all_gather(bias_rows, "row", axis=1, tiled=True)
    column_pair = lax.all_to_all(stacked, "row", split_axis=1, concat_axis=0, tiled=True)
    turned = jnp.swapaxes(column_pair, 0, 1)
    x_end = normed(turned, ln_gain[1])
    second_block = make_block(
        x_end, keep_mask, w_proj[1], w_tri[1], gate_bias[1], w_out[1], out_bias[1]
    )
    update_end = second_block(jnp.swapaxes(gathered, 1, 2), 0)
    return column_pair + jnp.swapaxes(update_end, 0, 1)


def solution(mesh):
    return jax.shard_map(
        local,
        mesh=mesh,
        in_specs=(P(("group", "row"), None, None), P("group"), P(), P(), P(), P(), P(), P()),
        out_specs=P("group", "row", None),
        check_vma=False,
    )
```

profile of v0, /device:TPU:1, one launch (start us, length us, event | category | flops | bytes accessed | tf_op | source)
XLA Modules:
  0.0 82.6 jit_solution(4775498775942339550)
XLA Ops:
  0.0 2.1 %copy.79 = f32[8,128,128]{1,2,0:T(8,128)} copy(f32[8,128,128]{2,1,0:T(8,128)} %param.8) | data formatting | bytes 1048576 | tf_op args[0]
  2.1 1.2 %reduce_sum.72 = f32[8,128]{1,0:T(8,128)S(1)} reduce(f32[8,128,128]{2,1,0:T(8,128)} %param.8, f32[]{:T(128)} %constant.12.clone.1), dimensions={2}, to_apply=%region_0.0 | reduce | flops 130048 | bytes 528388 | tf_op jit(solution)/shard_map/reduce_sum | solution.py:8
  3.4 1.4 %multiply_reduce_fusion.2 = f32[8,128]{1,0:T(8,128)S(1)} fusion(f32[8,128,128]{2,1,0:T(8,128)} %param.8, f32[8,128]{1,0:T(8,128)S(1)} %broadcast_multiply_fusion.2), kind=kLoop, calls=%fused_computation.50 | loop fusion | flops 392192 | bytes 532480 | tf_op jit(solution)/shard_map/reduce_sum | solution.py:10
  4.9 0.5 fusion.67
  5.4 0.1 fusion.66
  5.5 0.8 %copy.73 = bf16[8,128,128]{1,2,0:T(8,128)(2,1)} copy(bf16[8,128,128]{2,1,0:T(8,128)(2,1)S(1)} %get-tuple-element.7) | data formatting | bytes 524288 | tf_op jit(solution)/shard_map/slice | solution.py:29
  6.4 0.8 %copy.72 = bf16[8,128,128]{1,2,0:T(8,128)(2,1)} copy(bf16[8,128,128]{2,1,0:T(8,128)(2,1)S(1)} %fusion.23) | data formatting | bytes 524288 | tf_op jit(solution)/shard_map/convert_element_type | solution.py:28
  7.3 0.5 fusion.7
  7.7 23.3 %all_gather.6 = bf16[4,128,128]{2,0,1:T(4,128)(2,1)S(1)} all-gather(bf16[4,8,128]{2,0,1:T(4,128)(2,1)S(1)} %fusion.7), channel_id=1, replica_groups=mesh['group'=2,'row'=16] {'row'}, dimensions={1}, use_global_device_ids=true | all-gather | bytes 139264 | tf_op jit(solution)/shard_map/all_gather | solution.py:69
  31.1 0.1 copy.75
  31.4 0.9 %copy.71 = bf16[8,128,128]{1,2,0:T(8,128)(2,1)} copy(bf16[8,128,128]{2,1,0:T(8,128)(2,1)S(1)} %get-tuple-element.8) | data formatting | bytes 524288 | tf_op jit(solution)/shard_map/slice | solution.py:31
  32.2 3.3 %fusion.68 = (f32[8,4,128]{2,1,0:T(4,128)S(1)}, f32[8,4,128,128]{2,3,1,0:T(8,128)}) fusion(f32[4,128,128]{1,2,0:T(8,128)S(1)} %copy.75, pred[8,128]{1,0:T(8,128)(4,1)S(1)} %multiply_compare_fusion, bf16[8,128,4,32]{1,3,2,0:T(8,128)(2,1)} %bitcast.91, bf16[8,128,4,32]{1,3,2,0:T(8,128)(2,1)S(1)} %bitcast.90), kind=kOutput, calls=%fused_computation.101 | convolution fusion | flops 35651712 | bytes 2900992 | tf_op jit(solution)/shard_map/sub | solution.py:45
  35.5 2.1 %fusion.13 = f32[8,4,32,128]{3,2,1,0:T(8,128)S(1)} fusion(bf16[8,128,4,32]{1,3,2,0:T(8,128)(2,1)} %bitcast.95, f32[8,4,128,128]{2,3,1,0:T(8,128)} %get-tuple-element.18, f32[8,4,128]{2,1,0:T(4,128)S(1)} %get-tuple-element.17), kind=kOutput, calls=%fused_computation.23 | convolution fusion | flops 34603008 | bytes 2899968 | tf_op jit(solution)/shard_map/ihjk,ikhd->ijhd/dot_general | solution.py:47
  37.7 1.0 %copy.77 = f32[8,128,128]{2,1,0:T(8,128)} copy(f32[8,128,128]{1,2,0:T(8,128)S(1)} %bitcast.88) | data formatting | bytes 1048576 | tf_op jit(solution)/shard_map/reshape | solution.py:50
  38.7 1.4 %fusion.70 = (f32[8,128]{1,0:T(8,128)S(1)}, f32[8,128,128]{1,2,0:T(8,128)S(1)}) fusion(f32[8,128,128]{1,2,0:T(8,128)S(1)} %copy-done.1, f32[128]{0:T(128)S(1)} %get-tuple-element.12, bf16[2,128,128]{2,1,0:T(8,128)(2,1)S(1)} %copy-done.10, f32[8,128,128]{2,1,0:T(8,128)} %copy.77, f32[8,128,512]{2,1,0:T(8,128)S(1)} %get-tuple-element.16, ...), kind=kOutput, calls=%fused_computation.103 | convolution fusion | flops 34733056 | bytes 2135040 | tf_op jit(solution)/shard_map/ijc,cd->ijd/dot_general | solution.py:53
  40.1 1.0 %copy.80 = f32[8,128,128]{2,0,1:T(8,128)} copy(f32[8,128,128]{1,2,0:T(8,128)S(1)} %get-tuple-element.22) | data formatting | bytes 1048576 | tf_op jit(solution)/shard_map/add | solution.py:71
  41.1 3.5 %all-to-all-start = ((f32[8,128,128]{2,0,1:T(8,128)}), f32[8,128,128]{2,0,1:T(8,128)S(1)}, u32[]{:S(2)}, u32[]{:S(2)}) async-start(f32[8,128,128]{2,0,1:T(8,128)} %copy.80), calls=%async_computation | async-start | bytes 1048576 | tf_op jit(solution)/shard_map/all_to_all | solution.py:74
  44.7 0.2 fusion.8
  44.9 25.0 %all_gather.7 = bf16[4,128,128]{2,0,1:T(4,128)(2,1)S(1)} all-gather(bf16[4,8,128]{2,0,1:T(4,128)(2,1)S(1)} %fusion.8), channel_id=1, replica_groups=mesh['group'=2,'row'=16] {'row'}, dimensions={1}, use_global_device_ids=true | all-gather | bytes 139264 | tf_op jit(solution)/shard_map/all_gather | solution.py:73
  70.0 0.7 copy.89
  70.7 0.1 copy.82
  70.8 0.2 copy.83
  71.1 0.5 fusion.69
  71.7 0.1 fusion.65
  71.8 0.9 %copy.87 = bf16[8,128,128]{1,2,0:T(8,128)(2,1)} copy(bf16[8,128,128]{2,1,0:T(8,128)(2,1)S(1)} %get-tuple-element.5) | data formatting | bytes 524288 | tf_op jit(solution)/shard_map/slice | solution.py:29
  72.8 0.9 %copy.86 = bf16[8,128,128]{1,2,0:T(8,128)(2,1)} copy(bf16[8,128,128]{2,1,0:T(8,128)(2,1)S(1)} %fusion.17) | data formatting | bytes 524288 | tf_op jit(solution)/shard_map/convert_element_type | solution.py:28
  73.6 0.2 copy.85
  73.8 3.4 %fusion.71 = (f32[8,4,128]{2,1,0:T(4,128)S(1)}, f32[8,4,128,128]{2,3,1,0:T(8,128)}) fusion(f32[4,128,128]{1,2,0:T(8,128)S(1)} %copy-done.4, pred[8,128]{1,0:T(8,128)(4,1)S(1)} %multiply_compare_fusion, bf16[8,128,4,32]{1,3,2,0:T(8,128)(2,1)} %bitcast.93, bf16[8,128,4,32]{1,3,2,0:T(8,128)(2,1)} %bitcast.92), kind=kOutput, calls=%fused_computation.104 | convolution fusion | flops 35651712 | bytes 2900992 | tf_op jit(solution)/shard_map/sub | solution.py:45
  77.2 2.8 %fusion.14 = f32[8,4,32,128]{3,2,1,0:T(8,128)} fusion(bf16[8,128,4,32]{1,3,2,0:T(8,128)(2,1)S(1)} %bitcast.94, f32[8,4,128,128]{2,3,1,0:T(8,128)} %get-tuple-element.24, f32[8,4,128]{2,1,0:T(4,128)S(1)} %get-tuple-element.23), kind=kOutput, calls=%fused_computation.24 | convolution fusion | flops 34603008 | bytes 2899968 | tf_op jit(solution)/shard_map/ihjk,ikhd->ijhd/dot_general | solution.py:47
  80.0 1.2 %copy.91 = f32[8,128,128]{2,1,0:T(8,128)S(1)} copy(f32[8,128,128]{1,2,0:T(8,128)} %bitcast.89) | data formatting | bytes 1048576 | tf_op jit(solution)/shard_map/reshape | solution.py:50
  81.2 0.3 fusion.6
  81.5 1.1 %copy.93 = f32[128,8,128]{2,1,0:T(8,128)} copy(f32[128,8,128]{2,0,1:T(8,128)S(1)} %fusion.6) | data formatting | bytes 1048576 | tf_op jit(solution)/shard_map/add | solution.py:81
  (40 shorter events, 0.6 us)
Async XLA Ops:
  0.0 4.8 %copy-start = (f32[8,128,128]{2,1,0:T(8,128)S(1)}, f32[8,128,128]{2,1,0:T(8,128)}, u32[]{:S(2)}) copy-start(f32[8,128,128]{2,1,0:T(8,128)} %param.8) | copy-start | bytes 1572868
  0.0 4.8 %copy-start.6 = (f32[2,128]{1,0:T(2,128)S(1)}, f32[2,128]{1,0:T(2,128)}, u32[]{:S(2)}) copy-start(f32[2,128]{1,0:T(2,128)} %param.10) | copy-start | bytes 3076
  0.0 4.9 %copy-start.2 = (bf16[2,128,512]{2,1,0:T(8,128)(2,1)S(1)}, bf16[2,128,512]{2,1,0:T(8,128)(2,1)}, u32[]{:S(2)}) copy-start(bf16[2,128,512]{2,1,0:T(8,128)(2,1)} %param.11) | copy-start | bytes 786436
  5.4 1.9 %copy-start.5 = (bf16[2,128,4]{1,2,0:T(4,128)(2,1)S(1)}, bf16[2,128,4]{1,2,0:T(4,128)(2,1)}, u32[]{:S(2)}) copy-start(bf16[2,128,4]{1,2,0:T(4,128)(2,1)} %param.12) | copy-start | bytes 6148
  5.4 25.8 %copy-start.9 = (s32[128]{0:T(128)S(1)}, s32[128]{0:T(128)}, u32[]{:S(2)}) copy-start(s32[128]{0:T(128)} %param.9) | copy-start | bytes 1540
  7.3 25.0 %copy-start.3 = (bf16[8,128,128]{1,2,0:T(8,128)(2,1)S(1)}, bf16[8,128,128]{1,2,0:T(8,128)(2,1)}, u32[]{:S(2)}) copy-start(bf16[8,128,128]{1,2,0:T(8,128)(2,1)} %copy.73) | copy-start | bytes 786436
  35.5 3.2 %copy-start.7 = (f32[2,128]{1,0:T(2,128)S(1)}, f32[2,128]{1,0:T(2,128)}, u32[]{:S(2)}) copy-start(f32[2,128]{1,0:T(2,128)} %param.15) | copy-start | bytes 3076
  35.5 3.2 %copy-start.8 = (f32[2,128]{1,0:T(2,128)S(1)}, f32[2,128]{1,0:T(2,128)}, u32[]{:S(2)}) copy-start(f32[2,128]{1,0:T(2,128)} %param.13) | copy-start | bytes 3076
  35.5 3.2 %copy-start.1 = (f32[8,128,128]{1,2,0:T(8,128)S(1)}, f32[8,128,128]{1,2,0:T(8,128)}, u32[]{:S(2)}) copy-start(f32[8,128,128]{1,2,0:T(8,128)} %copy.79) | copy-start | bytes 1572868
  35.5 3.2 %copy-start.10 = (bf16[2,128,128]{2,1,0:T(8,128)(2,1)S(1)}, bf16[2,128,128]{2,1,0:T(8,128)(2,1)}, u32[]{:S(2)}) copy-start(bf16[2,128,128]{2,1,0:T(8,128)(2,1)} %param.14) | copy-start | bytes 196612
  41.1 29.6 %all-to-all-start = ((f32[8,128,128]{2,0,1:T(8,128)}), f32[8,128,128]{2,0,1:T(8,128)S(1)}, u32[]{:S(2)}, u32[]{:S(2)}) async-start(f32[8,128,128]{2,0,1:T(8,128)} %copy.80), calls=%async_computation | async-start | bytes 1048576 | tf_op jit(solution)/shard_map/all_to_all | solution.py:74
  71.7 2.1 %copy-start.4 = (f32[4,128,128]{1,2,0:T(8,128)S(1)}, f32[4,128,128]{1,2,0:T(8,128)}, u32[]{:S(2)}) copy-start(f32[4,128,128]{1,2,0:T(8,128)} %copy.89) | copy-start | bytes 786436
where the time goes:
time: 83.3 us; the launch traced here: 82.6 us
  blocking collectives  48.3 us (58%)
  matrix products  14.9 us (18%)
  local copies, waits for them, and re-layouts  12.5 us (15%)
  starting transfers between devices  3.53 us (4%)
  other arithmetic  3.12 us (4%)
    all_gather x1, blocking collectives, local(): gathered = lax.all_gather(bias_rows, 'row', axis=1, tiled=True)  25 us
    all_gather x1, blocking collectives, local(): lax.all_gather(tri_bias(x_start, w_tri[0]), 'row', axis=1, tiled=True)  23.3 us
    sub x2, matrix products, block(): weights = jnp.exp(scores - row_max)  6.62 us
    dot_general x2, matrix products, block(): jnp.einsum('ihjk,ikhd->ijhd', probabilities, values, preferred_element_ty...  4.91 us
    all_to_all x1, starting transfers between devices, local(): lax.all_to_all(stacked, 'row', split_axis=1, concat_axis=0, tiled=True)  3.53 us
    reshape x2, local copies, waits for them, and re-layouts, block(): mixture = mixture.reshape(local_rows, block_len, inner_width)  2.23 us
    unnamed x23, local copies, waits for them, and re-layouts  2.16 us
    slice x4, local copies, waits for them, and re-layouts, make_block(): key_rows = projected[..., inner_width:2 * inner_width].astype(jnp.bfloat16)  1.97 us
  transfers between devices with their start and end apart: 1, of which 0 were waited for; matrix products, arithmetic and copies ran while one was open for 1% of the time, Pallas kernels for 0%

commit v1 on v0

v1 whole, which is shorter than its diff:
```python
import functools

import jax
import jax.numpy as jnp
from jax import lax
from jax.experimental import pallas as pl
from jax.experimental.pallas import tpu as pltpu
from jax.sharding import PartitionSpec as P

LANES = 128
VMEM_BYTES = 24 * 2**20
EARLY_BYTES = 4 * 2**20
F32 = jnp.float32
BF16 = jnp.bfloat16
MASKED = -1000000000.0
LOG2E = 1.4426950408889634


def dot(a, b, dims=((1,), (0,))):
    return lax.dot_general(a, b, (dims, ((), ())), preferred_element_type=F32)


def interleave(streams, lag):
    waiting = [(i * lag, stream) for i, stream in enumerate(streams)]
    turn = 0
    while waiting:
        left = []
        for start, stream in waiting:
            if start <= turn and next(stream, waiting) is waiting:
                continue
            left.append((start, stream))
        waiting = left
        turn += 1


def normed(x, gain):
    centre = jnp.mean(x, axis=-1, keepdims=True)
    shifted = x - centre
    spread = jnp.mean(shifted * shifted, axis=-1, keepdims=True)
    return (shifted * lax.rsqrt(spread + 1e-05) * gain).astype(BF16)


def head_masks(heads, width):
    dim = width // heads
    down = lax.broadcasted_iota(jnp.int32, (width, LANES), 0) // dim
    across = lax.broadcasted_iota(jnp.int32, (LANES, width), 1) // dim
    return (
        [(down == h).astype(F32).astype(BF16) for h in range(heads)],
        [(across == h).astype(F32).astype(BF16) for h in range(heads)],
    )


def key_block(kt, picked, down):
    spread = []
    for h in picked:
        for t in range(kt.shape[1] // LANES):
            spread.append(kt[:, t * LANES : (t + 1) * LANES] * down[h])
    return jnp.concatenate(spread, axis=1)


def value_block(v, picked, across):
    parts = []
    for h in picked:
        for t in range(v.shape[0] // LANES):
            piece = v[t * LANES : (t + 1) * LANES] * across[h]
            parts.append(jnp.concatenate([piece, across[h]], axis=1))
    return jnp.concatenate(parts, axis=0)


def softened(scores, kept):
    part = jnp.where(kept, scores, F32(MASKED))
    return jnp.exp2(part - jnp.max(part, axis=1, keepdims=True)).astype(BF16)


def pairs_of(heads):
    return [tuple(range(h, min(h + 2, heads))) for h in range(0, heads, 2)]


def bias_kernel(x_ref, gain_ref, w_tri_ref, send_ref, norm_ref, rows_ref, held_ref, sems):
    rows, length, _ = x_ref.shape
    heads = w_tri_ref.shape[1]
    copies = [pltpu.make_async_copy(x_ref.at[i], held_ref.at[i], sems.at[i]) for i in range(rows)]
    for copy in copies:
        copy.start()

    def stream(i, t):
        span = slice(t * LANES, (t + 1) * LANES)
        if t == 0:
            copies[i].wait()
        x = held_ref[i, span, :]
        shifted = x - jnp.mean(x, axis=-1, keepdims=True)
        yield
        spread = jnp.mean(shifted * shifted, axis=-1, keepdims=True)
        yield
        x = (shifted * lax.rsqrt(spread + 1e-05) * gain_ref[0:1, :]).astype(BF16)
        norm_ref[i, span, :] = x
        yield
        rows_ref[pl.ds(t * heads * rows + i, heads, stride=rows), :] = dot(w_tri_ref[0], x, ((1,), (1,)))

    interleave([stream(i, t) for i in range(rows) for t in range(length // LANES)], 1)
    packed = rows_ref[...].astype(BF16)
    for d in range(send_ref.shape[0]):
        send_ref[d] = packed


def project_kernel(heads, early, norm_ref, flag_ref, mask_ref, w_ref, gate_bias_ref, *out_refs):
    q_ref, k_ref, v_ref, g_ref, keep_ref = out_refs[:5]
    rows, length, width = q_ref.shape
    scaling = (width // heads) ** (-0.5)
    down, _ = head_masks(heads, width)
    w = w_ref[0]
    w_keys = w[:, width : 2 * width].T
    first = lax.axis_index("row") * rows

    def stream(i):
        x = norm_ref[i]
        q = (dot(x, w[:, :width]) * scaling).astype(BF16)
        q_ref[i] = q
        kt = dot(w_keys, x, ((1,), (1,))).astype(BF16)
        k_ref[i] = kt
        yield
        v_ref[i] = dot(x, w[:, 2 * width : 3 * width]).astype(BF16)
        g_ref[i] = jax.nn.sigmoid(dot(x, w[:, 3 * width :]) + gate_bias_ref[0:1, :])
        keep_ref[i : i + 1, :] = mask_ref[...] * flag_ref[first + i]
        yield
        if early:
            for picked in pairs_of(heads):
                at = slice(picked[0] * length, (picked[-1] + 1) * length)
                out_refs[5][i, :, at] = dot(q, key_block(kt, picked, down)) * LOG2E
                yield

    interleave([stream(i) for i in range(rows)], 2)


def first_kernel(
    early, x_ref, q_ref, k_ref, v_ref, g_ref, got_ref, keep_ref, gain_ref, w_tri_ref, w_out_ref, out_bias_ref,
    *more_refs,
):
    send_ref, bias_ref, rows_ref = more_refs[-3:]
    rows, length, width = q_ref.shape
    heads = w_tri_ref.shape[1]
    parties = send_ref.shape[0]
    share = length // parties
    blocks = length // LANES
    for h in range(heads):
        for t in range(blocks):
            at = (t * heads + h) * rows
            bias_ref[:, h * length + t * LANES : h * length + (t + 1) * LANES] = (
                got_ref[:, at : at + rows, :].astype(F32).reshape(length, LANES) * LOG2E
            )
    down, across = head_masks(heads, width)

    def stream(i, t):
        span = slice(t * LANES, (t + 1) * LANES)
        kept = jnp.broadcast_to(keep_ref[i : i + 1, :], (LANES, length)) > 0
        both = None
        for picked in pairs_of(heads):
            weights = []
            scores = None
            if not early:
                scores = dot(q_ref[i, span, :], key_block(k_ref[i], picked, down)) * LOG2E
            for n, h in enumerate(picked):
                at = slice(h * length, (h + 1) * length)
                part = more_refs[0][i, span, at] if early else scores[:, n * length : (n + 1) * length]
                weights.append(softened(part + bias_ref[span, at], kept))
                yield
            term = dot(jnp.concatenate(weights, axis=1), value_block(v_ref[i], picked, across))
            both = term if both is None else both + term
            yield
        joined = (g_ref[i, span, :] * (both[:, :width] / both[:, width:])).astype(BF16)
        stacked = x_ref[i, span, :] + (dot(joined, w_out_ref[0]) + out_bias_ref[0:1, :])
        reach = LANES // share
        send_ref[t * reach : (t + 1) * reach, i * share : (i + 1) * share, :] = stacked.reshape(
            reach, share, stacked.shape[1]
        ).astype(BF16)
        yield
        shifted = stacked - jnp.mean(stacked, axis=-1, keepdims=True)
        yield
        spread = jnp.mean(shifted * shifted, axis=-1, keepdims=True)
        yield
        x = (shifted * lax.rsqrt(spread + 1e-05) * gain_ref[1:2, :]).astype(BF16)
        rows_ref[pl.ds(t * heads * rows + i, heads, stride=rows), :] = dot(w_tri_ref[0], x, ((1,), (1,)))

    interleave([stream(i, t) for i in range(rows) for t in range(blocks)], LAG)
    packed = rows_ref[...].astype(BF16)
    for d in range(parties):
        send_ref[d, rows * share :, :] = packed


def second_kernel(
    rows, got_ref, keep_ref, gain_ref, w_ref, gate_bias_ref, w_out_ref, out_bias_ref,
    out_ref, held_ref, bias_ref,
):
    parties = got_ref.shape[0]
    length = keep_ref.shape[1]
    share = length // parties
    blocks = length // LANES
    width = w_ref.shape[2] // 4
    heads = bias_ref.shape[1] // length
    scaling = (width // heads) ** (-0.5) * LOG2E
    held_ref[...] = got_ref[:, : rows * share, :].astype(F32).reshape(held_ref.shape)
    for h in range(heads):
        for t in range(blocks):
            at = rows * share + (t * heads + h) * rows
            turned = got_ref[:, at : at + rows, :].astype(F32).reshape(length, LANES)
            bias_ref[t * LANES : (t + 1) * LANES, h * length : (h + 1) * length] = turned.T * LOG2E
    down, across = head_masks(heads, width)
    w = w_ref[0]
    w_keys = w[:, width : 2 * width].T

    def stream(j):
        x = held_ref[pl.ds(j, length, stride=share), :]
        shifted = x - jnp.mean(x, axis=-1, keepdims=True)
        yield
        spread = jnp.mean(shifted * shifted, axis=-1, keepdims=True)
        yield
        x = (shifted * lax.rsqrt(spread + 1e-05) * gain_ref[1:2, :]).astype(BF16)
        q = (dot(x, w[:, :width]) * scaling).astype(BF16)
        kt = dot(w_keys, x, ((1,), (1,))).astype(BF16)
        yield
        v = dot(x, w[:, 2 * width : 3 * width]).astype(BF16)
        g = jax.nn.sigmoid(dot(x, w[:, 3 * width :]) + gate_bias_ref[1:2, :])
        yield
        for t in range(blocks):
            span = slice(t * LANES, (t + 1) * LANES)
            kept = jnp.broadcast_to(keep_ref[j : j + 1, :], (LANES, length)) > 0
            both = None
            for picked in pairs_of(heads):
                weights = []
                scores = dot(q[span], key_block(kt, picked, down))
                for n, h in enumerate(picked):
                    at = slice(h * length, (h + 1) * length)
                    part = scores[:, n * length : (n + 1) * length]
                    weights.append(softened(part + bias_ref[span, at], kept))
                    yield
                term = dot(jnp.concatenate(weights, axis=1), value_block(v, picked, across))
                both = term if both is None else both + term
                yield
            joined = (g[span] * (both[:, :width] / both[:, width:])).astype(BF16)
            update = dot(joined, w_out_ref[0]) + out_bias_ref[1:2, :]
            at = pl.ds(t * LANES * share + j, LANES, stride=share)
            out_ref[at, :] = held_ref[at, :] + update
            yield

    interleave([stream(j) for j in range(share)], LAG)


LAG = 3


def of_pass(array, p):
    shape = (1,) + array.shape[1:]
    return pl.BlockSpec(shape, lambda *_: (p,) + (0,) * (len(shape) - 1))


SMEM = pl.BlockSpec(memory_space=pltpu.SMEM)


def params():
    return pltpu.CompilerParams(vmem_limit_bytes=VMEM_BYTES)


def local(parties, pair_rep, token_mask, ln_gain, w_proj, w_tri, gate_bias, w_out, out_bias):
    rows, length, channels = pair_rep.shape
    heads = w_tri.shape[2]
    width = w_proj.shape[2] // 4
    share = length // parties
    bias_rows = length // LANES * heads * rows
    early = rows * length * heads * length * 4 <= EARLY_BYTES
    mask = token_mask.reshape(1, length)
    w_tri = jnp.swapaxes(w_tri, 1, 2)
    shape = jax.ShapeDtypeStruct

    def full(array):
        return pl.BlockSpec(array.shape, lambda *_: (0,) * array.ndim)

    send, norm = pl.pallas_call(
        bias_kernel,
        grid=(1,),
        out_shape=(
            shape((parties, bias_rows, LANES), BF16),
            shape((rows, length, channels), BF16),
        ),
        in_specs=[pl.BlockSpec(memory_space=pltpu.HBM), full(ln_gain), of_pass(w_tri, 0)],
        scratch_shapes=[
            pltpu.VMEM((bias_rows, LANES), F32),
            pltpu.VMEM(pair_rep.shape, F32),
            pltpu.SemaphoreType.DMA((rows,)),
        ],
        compiler_params=params(),
        name="bias",
    )(pair_rep, ln_gain, w_tri)
    got = lax.all_to_all(send, "row", split_axis=0, concat_axis=0, tiled=True)
    q, k, v, g, keep, *scores = pl.pallas_call(
        functools.partial(project_kernel, heads, early),
        grid=(1,),
        out_shape=(
            shape((rows, length, width), BF16),
            shape((rows, width, length), BF16),
            shape((rows, length, width), BF16),
            shape((rows, length, width), F32),
            shape((rows, length), jnp.int32),
        )
        + ((shape((rows, length, heads * length), F32),) if early else ()),
        in_specs=[full(norm), SMEM, full(mask), of_pass(w_proj, 0), full(gate_bias)],
        compiler_params=params(),
        cost_estimate=pl.CostEstimate(
            flops=2 * rows * length * channels * 4 * width,
            transcendentals=rows * length * width,
            bytes_accessed=rows * length * width * 12,
        ),
        name="project",
    )(norm, token_mask, mask, w_proj, gate_bias)
    taken = (pair_rep, q, k, v, g, got, keep, ln_gain)
    send = pl.pallas_call(
        functools.partial(first_kernel, early),
        grid=(1,),
        out_shape=shape((parties, rows * share + bias_rows, LANES), BF16),
        in_specs=[full(a) for a in taken]
        + [of_pass(w_tri, 1), of_pass(w_out, 0), full(out_bias)]
        + [full(a) for a in scores],
        scratch_shapes=[
            pltpu.VMEM((length, heads * length), F32),
            pltpu.VMEM((bias_rows, LANES), F32),
        ],
        compiler_params=params(),
        name="first",
    )(*taken, w_tri, w_out, out_bias, *scores)
    got = lax.all_to_all(send, "row", split_axis=0, concat_axis=0, tiled=True)
    out = pl.pallas_call(
        functools.partial(second_kernel, rows),
        grid=(1,),
        out_shape=shape((length * share, channels), F32),
        in_specs=[
            full(got), full(keep), full(ln_gain), of_pass(w_proj, 1), full(gate_bias), of_pass(w_out, 1),
            full(out_bias),
        ],
        scratch_shapes=[
            pltpu.VMEM((length * share, channels), F32),
            pltpu.VMEM((length, heads * length), F32),
        ],
        compiler_params=params(),
        name="second",
    )(got, keep, ln_gain, w_proj, gate_bias, w_out, out_bias)
    return out.reshape(length, share, channels)


def solution(mesh):
    return jax.shard_map(
        functools.partial(local, mesh.shape["row"]),
        mesh=mesh,
        in_specs=(P(("group", "row"), None, None), P("group"), P(), P(), P(), P(), P(), P()),
        out_specs=P("group", "row", None),
        check_vma=False,
    )
```

time: 83.3 us -> 49.1 us (0.59)
  blocking collectives: 48.3 us -> 16.4 us
  matrix products: 14.9 us -> 0 us
  Pallas kernels: 0 us -> 12.9 us
  starting transfers between devices: 3.53 us -> 7.34 us
  other arithmetic: 3.12 us -> 0 us
  local copies, waits for them, and re-layouts: 12.5 us -> 10.3 us
  waiting for transfers between devices: 0.01 us -> 1.29 us
    all_gather x2 -> x0, blocking collectives: 48.3 us -> none  [the longest x1 25 us: local(): gathered = lax.all_gather(bias_rows, 'row', axis=1, tiled=True)]
    all_to_all x0 -> x1, blocking collectives: none -> 16.4 us  [local(): got = lax.all_to_all(send, 'row', split_axis=0, concat_axis=0, tiled=True)]
    pallas_call x0 -> x4, Pallas kernels: none -> 12.9 us  [the longest x1 4.66 us: local(): pl.pallas_call(functools.partial(second_kernel, rows), grid=(1,), out_sha...]
    dot_general x8 -> x0, matrix products: 8.25 us -> none  [the longest x2 4.91 us: block(): jnp.einsum('ihjk,ikhd->ijhd', probabilities, values, preferred_element_ty...]
    unnamed x23 -> x32, local copies, waits for them, and re-layouts: 2.16 us -> 10.3 us
    sub x2 -> x0, matrix products: 6.62 us -> none  [block(): weights = jnp.exp(scores - row_max)]
    all_to_all x1, starting transfers between devices: 3.53 us -> 7.34 us  [local(): got = lax.all_to_all(send, 'row', split_axis=0, concat_axis=0, tiled=True)]
    slice x6 -> x0, local copies, waits for them, and re-layouts: 3.02 us -> none  [the longest x4 1.97 us: make_block(): key_rows = projected[..., inner_width:2 * inner_width].astype(jnp.bfloat16)]
  transfers between devices with their start and end apart: 1 -> 1, of which waited for: 0 -> 1; matrix products, arithmetic and copies ran while one was open for 1% -> 0% of each run, Pallas kernels for 0% -> 5%
where the time goes in v1:
time: 49.1 us; the launch traced here: 48.2 us
  blocking collectives  16.4 us (33%)
  Pallas kernels  12.9 us (26%)
  local copies, waits for them, and re-layouts  10.3 us (21%)
  starting transfers between devices  7.34 us (15%)
  waiting for transfers between devices  1.29 us (3%)
    all_to_all x1, blocking collectives, local(): got = lax.all_to_all(send, 'row', split_axis=0, concat_axis=0, tiled=True)  16.4 us
    unnamed x32, local copies, waits for them, and re-layouts  10.3 us
    all_to_all x1, starting transfers between devices, local(): got = lax.all_to_all(send, 'row', split_axis=0, concat_axis=0, tiled=True)  7.34 us
    pallas_call x1, Pallas kernels, local(): pl.pallas_call(functools.partial(second_kernel, rows), grid=(1,), out_sha...  4.66 us
    pallas_call x1, Pallas kernels, local(): pl.pallas_call(functools.partial(first_kernel, early), grid=(1,), out_sha...  3.03 us
    pallas_call x1, Pallas kernels, local(): pl.pallas_call(bias_kernel, grid=(1,), out_shape=(shape((parties, bias_ro...  2.91 us
    pallas_call x1, Pallas kernels, local(): pl.pallas_call(functools.partial(project_kernel, heads, early), grid=(1,)...  2.25 us
    all_to_all x1, waiting for transfers between devices, local(): got = lax.all_to_all(send, 'row', split_axis=0, concat_axis=0, tiled=True)  1.29 us
  transfers between devices with their start and end apart: 1, of which 1 were waited for; matrix products, arithmetic and copies ran while one was open for 0% of the time, Pallas kernels for 5%

profile of v1, /device:TPU:1, one launch (start us, length us, event | category | flops | bytes accessed | tf_op | source)
XLA Modules:
  0.0 48.2 jit_solution(9461760768938592300)
XLA Ops:
  0.0 0.0 copy-start
  0.0 1.0 %copy-done = f32[8,128,128]{2,1,0:T(8,128)S(1)} copy-done((f32[8,128,128]{2,1,0:T(8,128)S(1)}, f32[8,128,128]{2,1,0:T(8,128)}, u32[]{:S(2)}) %copy-start) | copy-done | bytes 524312
  1.0 0.0 copy-start.7
  1.0 0.7 %copy-done.7 = f32[2,128]{1,0:T(2,128)S(1)} copy-done((f32[2,128]{1,0:T(2,128)S(1)}, f32[2,128]{1,0:T(2,128)}, u32[]{:S(2)}) %copy-start.7) | copy-done | bytes 1048
  1.7 0.0 copy-start.10
  1.7 0.7 %copy-done.10 = bf16[2,128,4]{1,2,0:T(4,128)(2,1)S(1)} copy-done((bf16[2,128,4]{1,2,0:T(4,128)(2,1)S(1)}, bf16[2,128,4]{1,2,0:T(4,128)(2,1)}, u32[]{:S(2)}) %copy-start.10) | copy-done | bytes 2072
  2.4 2.9 %bias.1 = (bf16[16,32,128]{2,1,0:T(8,128)(2,1)}, bf16[8,128,128]{2,1,0:T(8,128)(2,1)S(1)}) custom-call(f32[8,128,128]{2,1,0:T(8,128)S(1)} %copy-done, f32[2,128]{1,0:T(2,128)S(1)} %copy-done.7, bf16[2,4,128]{2,1,0:T(4,128)(2,1)S(1)} %bitcast.3), custom_call_target="tpu_custom_call" | custom-call | tf_op jit(solution)/shard_map/bias/pallas_call | solution.py:277
  5.3 0.0 copy-start.5
  5.3 0.7 %copy-done.5 = bf16[8,128,128]{2,1,0:T(8,128)(2,1)} copy-done((bf16[8,128,128]{2,1,0:T(8,128)(2,1)}, bf16[8,128,128]{2,1,0:T(8,128)(2,1)S(1)}, u32[]{:S(2)}) %copy-start.5) | copy-done | bytes 262168
  6.0 7.3 %all-to-all-start = ((bf16[16,32,128]{2,1,0:T(8,128)(2,1)}), bf16[16,32,128]{2,1,0:T(8,128)(2,1)S(1)}, u32[]{:S(2)}, u32[]{:S(2)}) async-start(bf16[16,32,128]{2,1,0:T(8,128)(2,1)} %get-tuple-element.18), calls=%async_computation | async-start | bytes 262144 | tf_op jit(solution)/shard_map/all_to_all | solution.py:293
  13.4 0.0 copy-start.2
  13.4 0.9 %copy-done.2 = bf16[2,128,512]{2,1,0:T(8,128)(2,1)S(1)} copy-done((bf16[2,128,512]{2,1,0:T(8,128)(2,1)S(1)}, bf16[2,128,512]{2,1,0:T(8,128)(2,1)}, u32[]{:S(2)}) %copy-start.2) | copy-done | bytes 262168
  14.3 0.0 copy-start.6
  14.3 0.9 %copy-done.6 = bf16[8,128,128]{2,1,0:T(8,128)(2,1)S(1)} copy-done((bf16[8,128,128]{2,1,0:T(8,128)(2,1)S(1)}, bf16[8,128,128]{2,1,0:T(8,128)(2,1)}, u32[]{:S(2)}) %copy-start.6) | copy-done | bytes 262168
  15.3 0.0 copy-start.12
  15.3 0.7 %copy-done.12 = f32[2,128]{1,0:T(2,128)S(1)} copy-done((f32[2,128]{1,0:T(2,128)S(1)}, f32[2,128]{1,0:T(2,128)}, u32[]{:S(2)}) %copy-start.12) | copy-done | bytes 1048
  15.9 0.0 copy-start.15
  15.9 0.7 %copy-done.15 = s32[128]{0:T(128)S(1)} copy-done((s32[128]{0:T(128)S(1)}, s32[128]{0:T(128)}, u32[]{:S(2)}) %copy-start.15) | copy-done | bytes 536
  16.6 2.3 %project.1 = (bf16[8,128,128]{2,1,0:T(8,128)(2,1)S(1)}, bf16[8,128,128]{2,1,0:T(8,128)(2,1)S(1)}, bf16[8,128,128]{2,1,0:T(8,128)(2,1)S(1)}, f32[8,128,128]{2,1,0...) custom-call(bf16[8,128,128]{2,1,0:T(8,128)(2,1)S(1)} %copy-done.6, s32[128]{0:T(128)S(1)} %copy-done.15, ...), custom_call_target="tpu_custom_call" | custom-call | flops 134217728 | bytes 1572864 | tf_op jit(solution)/shard_map/project/pallas_call | solution.py:294
  18.9 1.3 %all-to-all-done.got_ref = bf16[16,32,128]{2,1,0:T(8,128)(2,1)S(1)} async-done(((bf16[16,32,128]{2,1,0:T(8,128)(2,1)}), bf16[16,32,128]{2,1,0:T(8,128)(2,1)S(1)}, u32[]{:S(2)}, u32[]{:S(2)}) %all-to-all-start) | async-done | bytes 131104 | tf_op jit(solution)/shard_map/all_to_all | solution.py:293
  20.2 0.0 copy-start.1
  20.2 1.0 %copy-done.1 = f32[8,128,128]{2,1,0:T(8,128)S(1)} copy-done((f32[8,128,128]{2,1,0:T(8,128)S(1)}, f32[8,128,128]{2,1,0:T(8,128)}, u32[]{:S(2)}) %copy-start.1) | copy-done | bytes 524312
  21.2 0.8 %copy-done.4 = bf16[2,128,128]{2,1,0:T(8,128)(2,1)S(1)} copy-done((bf16[2,128,128]{2,1,0:T(8,128)(2,1)S(1)}, bf16[2,128,128]{2,1,0:T(8,128)(2,1)}, u32[]{:S(2)}) %copy-start.4) | copy-done | bytes 65560
  22.0 0.7 %copy-done.8 = f32[2,128]{1,0:T(2,128)S(1)} copy-done((f32[2,128]{1,0:T(2,128)S(1)}, f32[2,128]{1,0:T(2,128)}, u32[]{:S(2)}) %copy-start.8) | copy-done | bytes 1048
  22.7 0.7 %copy-done.11 = bf16[2,128,4]{1,2,0:T(4,128)(2,1)S(1)} copy-done((bf16[2,128,4]{1,2,0:T(4,128)(2,1)S(1)}, bf16[2,128,4]{1,2,0:T(4,128)(2,1)}, u32[]{:S(2)}) %copy-start.11) | copy-done | bytes 2072
  23.4 0.7 %copy-done.14 = f32[2,128]{1,0:T(2,128)S(1)} copy-done((f32[2,128]{1,0:T(2,128)S(1)}, f32[2,128]{1,0:T(2,128)}, u32[]{:S(2)}) %copy-start.14) | copy-done | bytes 1048
  24.1 3.0 %first.1 = bf16[16,96,128]{2,1,0:T(8,128)(2,1)S(1)} custom-call(f32[8,128,128]{2,1,0:T(8,128)S(1)} %copy-done.1, bf16[8,128,128]{2,1,0:T(8,128)(2,1)S(1)} %get-tuple-element.14.q_ref, bf16[8,128,128]{2,1,0:T(8,128)(2,1)S(1)} %get-tuple-element.15.k_ref, bf16[8,128,128]{2,1,0:T(8,128)(2,1)S(1)} %get-tuple-element.16.v_ref, ...), custom_call_target="tpu_custom_call" | custom-call | tf_op jit(solution)/shard_map/first/pallas_call | solution.py:315
  27.1 16.4 %all_to_all.10.got_ref = bf16[16,96,128]{2,1,0:T(8,128)(2,1)S(1)} all-to-all(bf16[16,96,128]{2,1,0:T(8,128)(2,1)S(1)} %first.1), channel_id=1, replica_groups=mesh['group'=2,'row'=16] {'row'}, dimensions={0} | all-to-all | bytes 786432 | tf_op jit(solution)/shard_map/all_to_all | solution.py:329
  43.5 0.0 copy-done.3
  43.5 0.0 copy-done.9
  43.5 0.0 copy-done.13
  43.5 4.7 %second.1 = f32[1024,128]{1,0:T(8,128)} custom-call(bf16[16,96,128]{2,1,0:T(8,128)(2,1)S(1)} %all_to_all.10.got_ref, s32[8,128]{1,0:T(8,128)S(1)} %get-tuple-element.19.keep_ref, f32[2,128]{1,0:T(2,128)S(1)} %copy-done.9, bf16[2,128,512]{2,1,0:T(8,128)(2,1)S(1)} %copy-done.3, f32[2,128]{1,0:T(2,128)S(1)} %copy-done.13, bf16[2,128,128]{2,1,0:T(8,128)(2,1)S(1)} %copy-done.4, ...), custom_call_target="tpu_custom_call" | custom-call | tf_op jit(solution)/shard_map/second/pallas_call | solution.py:330
  (7 shorter events, 0.0 us)
Async XLA Ops:
  0.0 1.0 %copy-start = (f32[8,128,128]{2,1,0:T(8,128)S(1)}, f32[8,128,128]{2,1,0:T(8,128)}, u32[]{:S(2)}) copy-start(f32[8,128,128]{2,1,0:T(8,128)} %x_ref.3) | copy-start | bytes 1572868
  1.0 0.7 %copy-start.7 = (f32[2,128]{1,0:T(2,128)S(1)}, f32[2,128]{1,0:T(2,128)}, u32[]{:S(2)}) copy-start(f32[2,128]{1,0:T(2,128)} %gain_ref.5) | copy-start | bytes 3076
  1.7 0.7 %copy-start.10 = (bf16[2,128,4]{1,2,0:T(4,128)(2,1)S(1)}, bf16[2,128,4]{1,2,0:T(4,128)(2,1)}, u32[]{:S(2)}) copy-start(bf16[2,128,4]{1,2,0:T(4,128)(2,1)} %param.12) | copy-start | bytes 6148
  5.3 0.7 %copy-start.5 = (bf16[8,128,128]{2,1,0:T(8,128)(2,1)}, bf16[8,128,128]{2,1,0:T(8,128)(2,1)S(1)}, u32[]{:S(2)}) copy-start(bf16[8,128,128]{2,1,0:T(8,128)(2,1)S(1)} %get-tuple-element.13.norm_ref) | copy-start | bytes 786436
  6.0 14.1 %all-to-all-start = ((bf16[16,32,128]{2,1,0:T(8,128)(2,1)}), bf16[16,32,128]{2,1,0:T(8,128)(2,1)S(1)}, u32[]{:S(2)}, u32[]{:S(2)}) async-start(bf16[16,32,128]{2,1,0:T(8,128)(2,1)} %get-tuple-element.18), calls=%async_computation | async-start | bytes 262144 | tf_op jit(solution)/shard_map/all_to_all | solution.py:293
  13.4 0.9 %copy-start.2 = (bf16[2,128,512]{2,1,0:T(8,128)(2,1)S(1)}, bf16[2,128,512]{2,1,0:T(8,128)(2,1)}, u32[]{:S(2)}) copy-start(bf16[2,128,512]{2,1,0:T(8,128)(2,1)} %w_ref.3) | copy-start | bytes 786436
  14.3 0.9 %copy-start.6 = (bf16[8,128,128]{2,1,0:T(8,128)(2,1)S(1)}, bf16[8,128,128]{2,1,0:T(8,128)(2,1)}, u32[]{:S(2)}) copy-start(bf16[8,128,128]{2,1,0:T(8,128)(2,1)} %copy-done.5) | copy-start | bytes 786436
  15.3 0.7 %copy-start.12 = (f32[2,128]{1,0:T(2,128)S(1)}, f32[2,128]{1,0:T(2,128)}, u32[]{:S(2)}) copy-start(f32[2,128]{1,0:T(2,128)} %gate_bias_ref.3) | copy-start | bytes 3076
  15.9 0.7 %copy-start.15 = (s32[128]{0:T(128)S(1)}, s32[128]{0:T(128)}, u32[]{:S(2)}) copy-start(s32[128]{0:T(128)} %flag_ref.1) | copy-start | bytes 1540
  20.2 1.0 %copy-start.1 = (f32[8,128,128]{2,1,0:T(8,128)S(1)}, f32[8,128,128]{2,1,0:T(8,128)}, u32[]{:S(2)}) copy-start(f32[8,128,128]{2,1,0:T(8,128)} %x_ref.3) | copy-start | bytes 1572868
  21.2 0.8 %copy-start.4 = (bf16[2,128,128]{2,1,0:T(8,128)(2,1)S(1)}, bf16[2,128,128]{2,1,0:T(8,128)(2,1)}, u32[]{:S(2)}) copy-start(bf16[2,128,128]{2,1,0:T(8,128)(2,1)} %w_out_ref.3) | copy-start | bytes 196612
  22.0 0.7 %copy-start.8 = (f32[2,128]{1,0:T(2,128)S(1)}, f32[2,128]{1,0:T(2,128)}, u32[]{:S(2)}) copy-start(f32[2,128]{1,0:T(2,128)} %gain_ref.5) | copy-start | bytes 3076
  22.7 0.7 %copy-start.11 = (bf16[2,128,4]{1,2,0:T(4,128)(2,1)S(1)}, bf16[2,128,4]{1,2,0:T(4,128)(2,1)}, u32[]{:S(2)}) copy-start(bf16[2,128,4]{1,2,0:T(4,128)(2,1)} %param.12) | copy-start | bytes 6148
  23.4 0.7 %copy-start.14 = (f32[2,128]{1,0:T(2,128)S(1)}, f32[2,128]{1,0:T(2,128)}, u32[]{:S(2)}) copy-start(f32[2,128]{1,0:T(2,128)} %out_bias_ref.3) | copy-start | bytes 3076
  24.1 19.4 %copy-start.3 = (bf16[2,128,512]{2,1,0:T(8,128)(2,1)S(1)}, bf16[2,128,512]{2,1,0:T(8,128)(2,1)}, u32[]{:S(2)}) copy-start(bf16[2,128,512]{2,1,0:T(8,128)(2,1)} %w_ref.3) | copy-start | bytes 786436
  24.1 19.4 %copy-start.9 = (f32[2,128]{1,0:T(2,128)S(1)}, f32[2,128]{1,0:T(2,128)}, u32[]{:S(2)}) copy-start(f32[2,128]{1,0:T(2,128)} %gain_ref.5) | copy-start | bytes 3076
  24.1 19.4 %copy-start.13 = (f32[2,128]{1,0:T(2,128)S(1)}, f32[2,128]{1,0:T(2,128)}, u32[]{:S(2)}) copy-start(f32[2,128]{1,0:T(2,128)} %gate_bias_ref.3) | copy-start | bytes 3076

commit v2 on v1

--- a/solution.py
+++ b/solution.py
@@ -9,7 +9,9 @@
 
 LANES = 128
 VMEM_BYTES = 24 * 2**20
-EARLY_BYTES = 4 * 2**20
+EARLY_BYTES = 0
+KEPT = 3
+ALL_BYTES = 67 * 10**6
 F32 = jnp.float32
 BF16 = jnp.bfloat16
 MASKED = -1000000000.0
@@ -103,7 +105,8 @@
         send_ref[d] = packed
 
 
-def project_kernel(heads, early, norm_ref, flag_ref, mask_ref, w_ref, gate_bias_ref, *out_refs):
+def project_kernel(heads, early, norm_ref, flag_ref, mask_ref, w_ref, gate_bias_ref, *more_refs):
+    out_refs = more_refs[KEPT:]
     q_ref, k_ref, v_ref, g_ref, keep_ref = out_refs[:5]
     rows, length, width = q_ref.shape
     scaling = (width // heads) ** (-0.5)
@@ -245,7 +248,7 @@
     interleave([stream(j) for j in range(share)], LAG)
 
 
-LAG = 3
+LAG = 1
 
 
 def of_pass(array, p):
@@ -256,8 +259,8 @@
 SMEM = pl.BlockSpec(memory_space=pltpu.SMEM)
 
 
-def params():
-    return pltpu.CompilerParams(vmem_limit_bytes=VMEM_BYTES)
+def params(limit=VMEM_BYTES):
+    return pltpu.CompilerParams(vmem_limit_bytes=limit)
 
 
 def local(parties, pair_rep, token_mask, ln_gain, w_proj, w_tri, gate_bias, w_out, out_bias):
@@ -287,10 +290,11 @@
             pltpu.VMEM(pair_rep.shape, F32),
             pltpu.SemaphoreType.DMA((rows,)),
         ],
-        compiler_params=params(),
+        compiler_params=params(ALL_BYTES),
         name="bias",
     )(pair_rep, ln_gain, w_tri)
     got = lax.all_to_all(send, "row", split_axis=0, concat_axis=0, tiled=True)
+    kept = (w_tri, ln_gain, out_bias)
     q, k, v, g, keep, *scores = pl.pallas_call(
         functools.partial(project_kernel, heads, early),
         grid=(1,),
@@ -302,7 +306,7 @@
             shape((rows, length), jnp.int32),
         )
         + ((shape((rows, length, heads * length), F32),) if early else ()),
-        in_specs=[full(norm), SMEM, full(mask), of_pass(w_proj, 0), full(gate_bias)],
+        in_specs=[full(norm), SMEM, full(mask), of_pass(w_proj, 0), full(gate_bias)] + [full(a) for a in kept],
         compiler_params=params(),
         cost_estimate=pl.CostEstimate(
             flops=2 * rows * length * channels * 4 * width,
@@ -310,7 +314,7 @@
             bytes_accessed=rows * length * width * 12,
         ),
         name="project",
-    )(norm, token_mask, mask, w_proj, gate_bias)
+    )(norm, token_mask, mask, w_proj, gate_bias, *kept)
     taken = (pair_rep, q, k, v, g, got, keep, ln_gain)
     send = pl.pallas_call(
         functools.partial(first_kernel, early),

time: 49.1 us -> 39.9 us (0.81)
  local copies, waits for them, and re-layouts: 10.3 us -> 1.93 us
  Pallas kernels: 12.9 us -> 10.1 us
  waiting for transfers between devices: 1.29 us -> 3.76 us
  blocking collectives: 16.4 us -> 15.7 us
    unnamed x32 -> x20, local copies, waits for them, and re-layouts: 10.3 us -> 1.93 us
    all_to_all x1, waiting for transfers between devices: 1.29 us -> 3.76 us  [local(): got = lax.all_to_all(send, 'row', split_axis=0, concat_axis=0, tiled=True)]
    pallas_call x1, Pallas kernels: 4.66 us -> 3.24 us  [local(): pl.pallas_call(functools.partial(second_kernel, rows), grid=(1,), out_sha...]
    pallas_call x1, Pallas kernels: 2.25 us -> 1.07 us  [local(): pl.pallas_call(functools.partial(project_kernel, heads, early), grid=(1,)...]
    pallas_call x1, Pallas kernels: 3.03 us -> 1.97 us  [local(): pl.pallas_call(functools.partial(first_kernel, early), grid=(1,), out_sha...]
    pallas_call x1, Pallas kernels: 2.91 us -> 3.84 us  [local(): pl.pallas_call(bias_kernel, grid=(1,), out_shape=(shape((parties, bias_ro...]
    all_to_all x1, blocking collectives: 16.4 us -> 15.7 us  [local(): got = lax.all_to_all(send, 'row', split_axis=0, concat_axis=0, tiled=True)]
  transfers between devices with their start and end apart: 1 -> 1, of which waited for: 1 -> 1; matrix products, arithmetic and copies ran while one was open for 0% -> 0% of each run, Pallas kernels for 5% -> 3%
where the time goes in v2:
time: 39.9 us; the launch traced here: 39.1 us
  blocking collectives  15.7 us (39%)
  Pallas kernels  10.1 us (25%)
  starting transfers between devices  7.48 us (19%)
  waiting for transfers between devices  3.76 us (9%)
  local copies, waits for them, and re-layouts  1.93 us (5%)
    all_to_all x1, blocking collectives, local(): got = lax.all_to_all(send, 'row', split_axis=0, concat_axis=0, tiled=True)  15.7 us
    all_to_all x1, starting transfers between devices, local(): got = lax.all_to_all(send, 'row', split_axis=0, concat_axis=0, tiled=True)  7.48 us
    pallas_call x1, Pallas kernels, local(): pl.pallas_call(bias_kernel, grid=(1,), out_shape=(shape((parties, bias_ro...  3.84 us
    all_to_all x1, waiting for transfers between devices, local(): got = lax.all_to_all(send, 'row', split_axis=0, concat_axis=0, tiled=True)  3.76 us
    pallas_call x1, Pallas kernels, local(): pl.pallas_call(functools.partial(second_kernel, rows), grid=(1,), out_sha...  3.24 us
    pallas_call x1, Pallas kernels, local(): pl.pallas_call(functools.partial(first_kernel, early), grid=(1,), out_sha...  1.97 us
    unnamed x20, local copies, waits for them, and re-layouts  1.93 us
    pallas_call x1, Pallas kernels, local(): pl.pallas_call(functools.partial(project_kernel, heads, early), grid=(1,)...  1.07 us
  transfers between devices with their start and end apart: 1, of which 1 were waited for; matrix products, arithmetic and copies ran while one was open for 0% of the time, Pallas kernels for 3%

profile of v2, /device:TPU:1, one launch (start us, length us, event | category | flops | bytes accessed | tf_op | source)
XLA Modules:
  0.0 39.1 jit_solution(15632035044971716881)
XLA Ops:
  0.0 0.0 copy-start.5
  0.0 0.0 copy-start.6
  0.0 0.0 copy-start.7
  0.0 0.0 copy-start.8
  0.0 0.0 copy-start.9
  0.0 3.8 %bias.1 = (bf16[16,32,128]{2,1,0:T(8,128)(2,1)}, bf16[8,128,128]{2,1,0:T(8,128)(2,1)}) custom-call(f32[8,128,128]{2,1,0:T(8,128)} %x_ref.3, f32[2,128]{1,0:T(2,128)} %gain_ref.5, bf16[2,4,128]{2,1,0:T(4,128)(2,1)} %bitcast.3), custom_call_target="tpu_custom_call" | custom-call | tf_op jit(solution)/shard_map/bias/pallas_call | solution.py:280
  3.9 0.0 copy-start
  3.9 7.5 %all-to-all-start = ((bf16[16,32,128]{2,1,0:T(8,128)(2,1)}), bf16[16,32,128]{2,1,0:T(8,128)(2,1)S(1)}, u32[]{:S(2)}, u32[]{:S(2)}) async-start(bf16[16,32,128]{2,1,0:T(8,128)(2,1)} %get-tuple-element.17), calls=%async_computation | async-start | bytes 262144 | tf_op jit(solution)/shard_map/all_to_all | solution.py:296
  11.4 0.0 copy-done.5
  11.4 0.0 copy-done.6
  11.4 0.0 copy-done.7
  11.4 0.0 copy-done.8
  11.4 0.0 copy-done.9
  11.4 0.0 copy-start.1
  11.4 0.9 %copy-done.1 = bf16[2,128,512]{2,1,0:T(8,128)(2,1)S(1)} copy-done((bf16[2,128,512]{2,1,0:T(8,128)(2,1)S(1)}, bf16[2,128,512]{2,1,0:T(8,128)(2,1)}, u32[]{:S(2)}) %copy-start.1) | copy-done | bytes 262168
  12.4 0.0 copy-start.4
  12.4 0.9 %copy-done.4 = bf16[8,128,128]{2,1,0:T(8,128)(2,1)S(1)} copy-done((bf16[8,128,128]{2,1,0:T(8,128)(2,1)S(1)}, bf16[8,128,128]{2,1,0:T(8,128)(2,1)}, u32[]{:S(2)}) %copy-start.4) | copy-done | bytes 262168
  13.3 0.0 copy-start.3
  13.3 1.1 %project.1 = (bf16[8,128,128]{2,1,0:T(8,128)(2,1)S(1)}, bf16[8,128,128]{2,1,0:T(8,128)(2,1)S(1)}, bf16[8,128,128]{2,1,0:T(8,128)(2,1)S(1)}, f32[8,128,128]{2,1,0:T(8,128)S(1)}, s32[8,128]{1,0:T(8,128)S(1)}) custom-call(bf16[8,128,128]{2,1,0:T(8,128)(2,1)S(1)} %copy-done.4, s32[128]{0:T(128)S(1)} %copy-done.9, s32[1,128]{1,0:T(1,128)S(1)} %bitcast.6, ...), custom_call_target="tpu_custom_call" | custom-call | flops 134217728 | bytes 1572864 | tf_op jit(solution)/shard_map/project/pallas_call | solution.py:298
  14.4 3.8 %all-to-all-done.got_ref = bf16[16,32,128]{2,1,0:T(8,128)(2,1)S(1)} async-done(((bf16[16,32,128]{2,1,0:T(8,128)(2,1)}), bf16[16,32,128]{2,1,0:T(8,128)(2,1)S(1)}, u32[]{:S(2)}, u32[]{:S(2)}) %all-to-all-start) | async-done | bytes 131104 | tf_op jit(solution)/shard_map/all_to_all | solution.py:296
  18.2 0.0 copy-done
  18.2 0.0 copy-done.3
  18.2 2.0 %first.1 = bf16[16,96,128]{2,1,0:T(8,128)(2,1)S(1)} custom-call(f32[8,128,128]{2,1,0:T(8,128)S(1)} %copy-done, bf16[8,128,128]{2,1,0:T(8,128)(2,1)S(1)} %get-tuple-element.13.q_ref, bf16[8,128,128]{2,1,0:T(8,128)(2,1)S(1)} %get-tuple-element.14.k_ref, bf16[8,128,128]{2,1,0:T(8,128)(2,1)S(1)} %get-tuple-element.15.v_ref, ...), custom_call_target="tpu_custom_call" | custom-call | tf_op jit(solution)/shard_map/first/pallas_call | solution.py:319
  20.1 0.0 copy-start.2
  20.2 15.7 %all_to_all.10.got_ref = bf16[16,96,128]{2,1,0:T(8,128)(2,1)S(1)} all-to-all(bf16[16,96,128]{2,1,0:T(8,128)(2,1)S(1)} %first.1), channel_id=1, replica_groups=mesh['group'=2,'row'=16] {'row'}, dimensions={0} | all-to-all | bytes 786432 | tf_op jit(solution)/shard_map/all_to_all | solution.py:333
  35.9 0.0 copy-done.2
  35.9 3.2 %second.1 = f32[1024,128]{1,0:T(8,128)} custom-call(bf16[16,96,128]{2,1,0:T(8,128)(2,1)S(1)} %all_to_all.10.got_ref, s32[8,128]{1,0:T(8,128)S(1)} %get-tuple-element.18.keep_ref, f32[2,128]{1,0:T(2,128)S(1)} %copy-done.6, bf16[2,128,512]{2,1,0:T(8,128)(2,1)S(1)} %copy-done.2, f32[2,128]{1,0:T(2,128)S(1)} %copy-done.8, bf16[2,128,128]{2,1,0:T(8,128)(2,1)S(1)} %copy-done.3, ...), custom_call_target="tpu_custom_call" | custom-call | tf_op jit(solution)/shard_map/second/pallas_call | solution.py:334
Async XLA Ops:
  0.0 11.4 %copy-start.5 = (bf16[2,128,4]{1,2,0:T(4,128)(2,1)S(1)}, bf16[2,128,4]{1,2,0:T(4,128)(2,1)}, u32[]{:S(2)}) copy-start(bf16[2,128,4]{1,2,0:T(4,128)(2,1)} %param.12) | copy-start | bytes 6148
  0.0 11.4 %copy-start.6 = (f32[2,128]{1,0:T(2,128)S(1)}, f32[2,128]{1,0:T(2,128)}, u32[]{:S(2)}) copy-start(f32[2,128]{1,0:T(2,128)} %gain_ref.5) | copy-start | bytes 3076
  0.0 11.4 %copy-start.7 = (f32[2,128]{1,0:T(2,128)S(1)}, f32[2,128]{1,0:T(2,128)}, u32[]{:S(2)}) copy-start(f32[2,128]{1,0:T(2,128)} %out_bias_ref.3) | copy-start | bytes 3076
  0.0 11.4 %copy-start.8 = (f32[2,128]{1,0:T(2,128)S(1)}, f32[2,128]{1,0:T(2,128)}, u32[]{:S(2)}) copy-start(f32[2,128]{1,0:T(2,128)} %gate_bias_ref.3) | copy-start | bytes 3076
  0.0 11.4 %copy-start.9 = (s32[128]{0:T(128)S(1)}, s32[128]{0:T(128)}, u32[]{:S(2)}) copy-start(s32[128]{0:T(128)} %flag_ref.1) | copy-start | bytes 1540
  3.9 14.3 %copy-start = (f32[8,128,128]{2,1,0:T(8,128)S(1)}, f32[8,128,128]{2,1,0:T(8,128)}, u32[]{:S(2)}) copy-start(f32[8,128,128]{2,1,0:T(8,128)} %x_ref.3) | copy-start | bytes 1572868
  3.9 14.3 %all-to-all-start = ((bf16[16,32,128]{2,1,0:T(8,128)(2,1)}), bf16[16,32,128]{2,1,0:T(8,128)(2,1)S(1)}, u32[]{:S(2)}, u32[]{:S(2)}) async-start(bf16[16,32,128]{2,1,0:T(8,128)(2,1)} %get-tuple-element.17), calls=%async_computation | async-start | bytes 262144 | tf_op jit(solution)/shard_map/all_to_all | solution.py:296
  11.4 1.0 %copy-start.1 = (bf16[2,128,512]{2,1,0:T(8,128)(2,1)S(1)}, bf16[2,128,512]{2,1,0:T(8,128)(2,1)}, u32[]{:S(2)}) copy-start(bf16[2,128,512]{2,1,0:T(8,128)(2,1)} %w_ref.3) | copy-start | bytes 786436
  12.4 0.9 %copy-start.4 = (bf16[8,128,128]{2,1,0:T(8,128)(2,1)S(1)}, bf16[8,128,128]{2,1,0:T(8,128)(2,1)}, u32[]{:S(2)}) copy-start(bf16[8,128,128]{2,1,0:T(8,128)(2,1)} %get-tuple-element.12.norm_ref) | copy-start | bytes 786436
  13.3 4.8 %copy-start.3 = (bf16[2,128,128]{2,1,0:T(8,128)(2,1)S(1)}, bf16[2,128,128]{2,1,0:T(8,128)(2,1)}, u32[]{:S(2)}) copy-start(bf16[2,128,128]{2,1,0:T(8,128)(2,1)} %w_out_ref.3) | copy-start | bytes 196612
  20.1 15.7 %copy-start.2 = (bf16[2,128,512]{2,1,0:T(8,128)(2,1)S(1)}, bf16[2,128,512]{2,1,0:T(8,128)(2,1)}, u32[]{:S(2)}) copy-start(bf16[2,128,512]{2,1,0:T(8,128)(2,1)} %w_ref.3) | copy-start | bytes 786436

commit v3 on v2

--- a/solution.py
+++ b/solution.py
@@ -9,8 +9,7 @@
 
 LANES = 128
 VMEM_BYTES = 24 * 2**20
-EARLY_BYTES = 0
-KEPT = 3
+KEPT = 2
 ALL_BYTES = 67 * 10**6
 F32 = jnp.float32
 BF16 = jnp.bfloat16
@@ -78,26 +77,30 @@
     return [tuple(range(h, min(h + 2, heads))) for h in range(0, heads, 2)]
 
 
-def bias_kernel(x_ref, gain_ref, w_tri_ref, send_ref, norm_ref, rows_ref, held_ref, sems):
+def bias_kernel(x_ref, gain_ref, w_tri_ref, send_ref, rows_ref, held_ref, scale_ref, weight_ref, sems):
     rows, length, _ = x_ref.shape
     heads = w_tri_ref.shape[1]
     copies = [pltpu.make_async_copy(x_ref.at[i], held_ref.at[i], sems.at[i]) for i in range(rows)]
+    copies += [
+        pltpu.make_async_copy(gain_ref, scale_ref, sems.at[rows]),
+        pltpu.make_async_copy(w_tri_ref.at[0], weight_ref, sems.at[rows + 1]),
+    ]
     for copy in copies:
         copy.start()
+    copies[rows].wait()
+    copies[rows + 1].wait()
 
     def stream(i, t):
-        span = slice(t * LANES, (t + 1) * LANES)
         if t == 0:
             copies[i].wait()
-        x = held_ref[i, span, :]
+        x = held_ref[i, t * LANES : (t + 1) * LANES, :]
         shifted = x - jnp.mean(x, axis=-1, keepdims=True)
         yield
         spread = jnp.mean(shifted * shifted, axis=-1, keepdims=True)
         yield
-        x = (shifted * lax.rsqrt(spread + 1e-05) * gain_ref[0:1, :]).astype(BF16)
-        norm_ref[i, span, :] = x
-        yield
-        rows_ref[pl.ds(t * heads * rows + i, heads, stride=rows), :] = dot(w_tri_ref[0], x, ((1,), (1,)))
+        x = (shifted * lax.rsqrt(spread + 1e-05) * scale_ref[0:1, :]).astype(BF16)
+        yield
+        rows_ref[pl.ds(t * heads * rows + i, heads, stride=rows), :] = dot(weight_ref[...], x, ((1,), (1,)))
 
     interleave([stream(i, t) for i in range(rows) for t in range(length // LANES)], 1)
     packed = rows_ref[...].astype(BF16)
@@ -105,41 +108,35 @@
         send_ref[d] = packed
 
 
-def project_kernel(heads, early, norm_ref, flag_ref, mask_ref, w_ref, gate_bias_ref, *more_refs):
-    out_refs = more_refs[KEPT:]
-    q_ref, k_ref, v_ref, g_ref, keep_ref = out_refs[:5]
+def project_kernel(heads, x_ref, gain_ref, flag_ref, mask_ref, w_ref, gate_bias_ref, *more_refs):
+    q_ref, k_ref, v_ref, g_ref, keep_ref = more_refs[KEPT:]
     rows, length, width = q_ref.shape
-    scaling = (width // heads) ** (-0.5)
-    down, _ = head_masks(heads, width)
+    scaling = (width // heads) ** (-0.5) * LOG2E
     w = w_ref[0]
     w_keys = w[:, width : 2 * width].T
     first = lax.axis_index("row") * rows
 
     def stream(i):
-        x = norm_ref[i]
-        q = (dot(x, w[:, :width]) * scaling).astype(BF16)
-        q_ref[i] = q
-        kt = dot(w_keys, x, ((1,), (1,))).astype(BF16)
-        k_ref[i] = kt
+        x = x_ref[i]
+        shifted = x - jnp.mean(x, axis=-1, keepdims=True)
+        yield
+        spread = jnp.mean(shifted * shifted, axis=-1, keepdims=True)
+        yield
+        x = (shifted * lax.rsqrt(spread + 1e-05) * gain_ref[0:1, :]).astype(BF16)
+        q_ref[i] = (dot(x, w[:, :width]) * scaling).astype(BF16)
+        k_ref[i] = dot(w_keys, x, ((1,), (1,))).astype(BF16)
         yield
         v_ref[i] = dot(x, w[:, 2 * width : 3 * width]).astype(BF16)
         g_ref[i] = jax.nn.sigmoid(dot(x, w[:, 3 * width :]) + gate_bias_ref[0:1, :])
         keep_ref[i : i + 1, :] = mask_ref[...] * flag_ref[first + i]
-        yield
-        if early:
-            for picked in pairs_of(heads):
-                at = slice(picked[0] * length, (picked[-1] + 1) * length)
-                out_refs[5][i, :, at] = dot(q, key_block(kt, picked, down)) * LOG2E
-                yield
-
-    interleave([stream(i) for i in range(rows)], 2)
+
+    interleave([stream(i) for i in range(rows)], 1)
 
 
 def first_kernel(
-    early, x_ref, q_ref, k_ref, v_ref, g_ref, got_ref, keep_ref, gain_ref, w_tri_ref, w_out_ref, out_bias_ref,
-    *more_refs,
+    rank, x_ref, q_ref, k_ref, v_ref, g_ref, got_ref, keep_ref, gain_ref, w_tri_ref, w_out_ref, out_bias_ref,
+    send_ref, bias_ref, rows_ref,
 ):
-    send_ref, bias_ref, rows_ref = more_refs[-3:]
     rows, length, width = q_ref.shape
     heads = w_tri_ref.shape[1]
     parties = send_ref.shape[0]
@@ -148,9 +145,10 @@
     for h in range(heads):
         for t in range(blocks):
             at = (t * heads + h) * rows
-            bias_ref[:, h * length + t * LANES : h * length + (t + 1) * LANES] = (
-                got_ref[:, at : at + rows, :].astype(F32).reshape(length, LANES) * LOG2E
-            )
+            for s in range(parties):
+                bias_ref[s * rows : (s + 1) * rows, h * length + t * LANES : h * length + (t + 1) * LANES] = (
+                    got_ref[rank[s], at : at + rows, :].astype(F32) * LOG2E
+                )
     down, across = head_masks(heads, width)
 
     def stream(i, t):
@@ -159,12 +157,10 @@
         both = None
         for picked in pairs_of(heads):
             weights = []
-            scores = None
-            if not early:
-                scores = dot(q_ref[i, span, :], key_block(k_ref[i], picked, down)) * LOG2E
+            scores = dot(q_ref[i, span, :], key_block(k_ref[i], picked, down))
             for n, h in enumerate(picked):
                 at = slice(h * length, (h + 1) * length)
-                part = more_refs[0][i, span, at] if early else scores[:, n * length : (n + 1) * length]
+                part = scores[:, n * length : (n + 1) * length]
                 weights.append(softened(part + bias_ref[span, at], kept))
                 yield
             term = dot(jnp.concatenate(weights, axis=1), value_block(v_ref[i], picked, across))
@@ -173,9 +169,10 @@
         joined = (g_ref[i, span, :] * (both[:, :width] / both[:, width:])).astype(BF16)
         stacked = x_ref[i, span, :] + (dot(joined, w_out_ref[0]) + out_bias_ref[0:1, :])
         reach = LANES // share
-        send_ref[t * reach : (t + 1) * reach, i * share : (i + 1) * share, :] = stacked.reshape(
-            reach, share, stacked.shape[1]
-        ).astype(BF16)
+        for d in range(reach):
+            send_ref[rank[t * reach + d], i * share : (i + 1) * share, :] = stacked[
+                d * share : (d + 1) * share
+            ].astype(BF16)
         yield
         shifted = stacked - jnp.mean(stacked, axis=-1, keepdims=True)
         yield
@@ -191,7 +188,7 @@
 
 
 def second_kernel(
-    rows, got_ref, keep_ref, gain_ref, w_ref, gate_bias_ref, w_out_ref, out_bias_ref,
+    rows, rank, got_ref, keep_ref, gain_ref, w_ref, gate_bias_ref, w_out_ref, out_bias_ref,
     out_ref, held_ref, bias_ref,
 ):
     parties = got_ref.shape[0]
@@ -201,11 +198,14 @@
     width = w_ref.shape[2] // 4
     heads = bias_ref.shape[1] // length
     scaling = (width // heads) ** (-0.5) * LOG2E
-    held_ref[...] = got_ref[:, : rows * share, :].astype(F32).reshape(held_ref.shape)
+    for s in range(parties):
+        held_ref[s * rows * share : (s + 1) * rows * share, :] = got_ref[rank[s], : rows * share, :].astype(F32)
     for h in range(heads):
         for t in range(blocks):
             at = rows * share + (t * heads + h) * rows
-            turned = got_ref[:, at : at + rows, :].astype(F32).reshape(length, LANES)
+            turned = jnp.concatenate(
+                [got_ref[rank[s], at : at + rows, :].astype(F32) for s in range(parties)], axis=0
+            )
             bias_ref[t * LANES : (t + 1) * LANES, h * length : (h + 1) * length] = turned.T * LOG2E
     down, across = head_masks(heads, width)
     w = w_ref[0]
@@ -259,6 +259,14 @@
 SMEM = pl.BlockSpec(memory_space=pltpu.SMEM)
 
 
+def group_order(parties):
+    stride = max(parties // 4, 1)
+    middle = [2, 1, 3, 0]
+    order = [m * stride + k for k in range(stride) for m in middle if m * stride + k < parties]
+    lead = parties // 2 + (1 if parties > 2 else 0)
+    return [lead] + [d for d in order if d != lead]
+
+
 def params(limit=VMEM_BYTES):
     return pltpu.CompilerParams(vmem_limit_bytes=limit)
 
@@ -269,7 +277,6 @@
     width = w_proj.shape[2] // 4
     share = length // parties
     bias_rows = length // LANES * heads * rows
-    early = rows * length * heads * length * 4 <= EARLY_BYTES
     mask = token_mask.reshape(1, length)
     w_tri = jnp.swapaxes(w_tri, 1, 2)
     shape = jax.ShapeDtypeStruct
@@ -277,26 +284,32 @@
     def full(array):
         return pl.BlockSpec(array.shape, lambda *_: (0,) * array.ndim)
 
-    send, norm = pl.pallas_call(
+    order = group_order(parties)
+    rank = [order.index(d) for d in range(parties)]
+
+    def exchange(parts):
+        return lax.all_to_all(parts, "row", split_axis=0, concat_axis=0, tiled=True, axis_index_groups=[order])
+
+    hbm = pl.BlockSpec(memory_space=pltpu.HBM)
+    send = pl.pallas_call(
         bias_kernel,
         grid=(1,),
-        out_shape=(
-            shape((parties, bias_rows, LANES), BF16),
-            shape((rows, length, channels), BF16),
-        ),
-        in_specs=[pl.BlockSpec(memory_space=pltpu.HBM), full(ln_gain), of_pass(w_tri, 0)],
+        out_shape=shape((parties, bias_rows, LANES), BF16),
+        in_specs=[hbm, hbm, hbm],
         scratch_shapes=[
             pltpu.VMEM((bias_rows, LANES), F32),
             pltpu.VMEM(pair_rep.shape, F32),
-            pltpu.SemaphoreType.DMA((rows,)),
+            pltpu.VMEM(ln_gain.shape, F32),
+            pltpu.VMEM(w_tri.shape[1:], BF16),
+            pltpu.SemaphoreType.DMA((rows + 2,)),
         ],
         compiler_params=params(ALL_BYTES),
         name="bias",
     )(pair_rep, ln_gain, w_tri)
-    got = lax.all_to_all(send, "row", split_axis=0, concat_axis=0, tiled=True)
-    kept = (w_tri, ln_gain, out_bias)
-    q, k, v, g, keep, *scores = pl.pallas_call(
-        functools.partial(project_kernel, heads, early),
+    got = exchange(send)
+    kept = (w_tri, out_bias)
+    q, k, v, g, keep = pl.pallas_call(
+        functools.partial(project_kernel, heads),
         grid=(1,),
         out_shape=(
             shape((rows, length, width), BF16),
@@ -304,9 +317,9 @@
             shape((rows, length, width), BF16),
             shape((rows, length, width), F32),
             shape((rows, length), jnp.int32),
-        )
-        + ((shape((rows, length, heads * length), F32),) if early else ()),
-        in_specs=[full(norm), SMEM, full(mask), of_pass(w_proj, 0), full(gate_bias)] + [full(a) for a in kept],
+        ),
+        in_specs=[full(pair_rep), full(ln_gain), SMEM, full(mask), of_pass(w_proj, 0), full(gate_bias)]
+        + [full(a) for a in kept],
         compiler_params=params(),
         cost_estimate=pl.CostEstimate(
             flops=2 * rows * length * channels * 4 * width,
@@ -314,25 +327,24 @@
             bytes_accessed=rows * length * width * 12,
         ),
         name="project",
-    )(norm, token_mask, mask, w_proj, gate_bias, *kept)
+    )(pair_rep, ln_gain, token_mask, mask, w_proj, gate_bias, *kept)
     taken = (pair_rep, q, k, v, g, got, keep, ln_gain)
     send = pl.pallas_call(
-        functools.partial(first_kernel, early),
+        functools.partial(first_kernel, rank),
         grid=(1,),
         out_shape=shape((parties, rows * share + bias_rows, LANES), BF16),
         in_specs=[full(a) for a in taken]
-        + [of_pass(w_tri, 1), of_pass(w_out, 0), full(out_bias)]
-        + [full(a) for a in scores],
+        + [of_pass(w_tri, 1), of_pass(w_out, 0), full(out_bias)],
         scratch_shapes=[
             pltpu.VMEM((length, heads * length), F32),
             pltpu.VMEM((bias_rows, LANES), F32),
         ],
         compiler_params=params(),
         name="first",
-    )(*taken, w_tri, w_out, out_bias, *scores)
-    got = lax.all_to_all(send, "row", split_axis=0, concat_axis=0, tiled=True)
+    )(*taken, w_tri, w_out, out_bias)
+    got = exchange(send)
     out = pl.pallas_call(
-        functools.partial(second_kernel, rows),
+        functools.partial(second_kernel, rows, rank),
         grid=(1,),
         out_shape=shape((length * share, channels), F32),
         in_specs=[

time: 39.9 us -> 36.3 us (0.910)
  waiting for transfers between devices: 3.76 us -> 1.89 us
  blocking collectives: 15.7 us -> 14.9 us
    all_to_all x1, waiting for transfers between devices: 3.76 us -> 1.89 us  [exchange(): lax.all_to_all(parts, 'row', split_axis=0, concat_axis=0, tiled=True, axi...]
    all_to_all x1, blocking collectives: 15.7 us -> 14.9 us  [exchange(): lax.all_to_all(parts, 'row', split_axis=0, concat_axis=0, tiled=True, axi...]
    unnamed x20 -> x18, local copies, waits for them, and re-layouts: 1.93 us -> 1.69 us
  transfers between devices with their start and end apart: 1 -> 1, of which waited for: 1 -> 1; matrix products, arithmetic and copies ran while one was open for 0% -> 0% of each run, Pallas kernels for 3% -> 4%
where the time goes in v3:
time: 36.3 us; the launch traced here: 35.9 us
  blocking collectives  14.9 us (41%)
  Pallas kernels  9.99 us (28%)
  starting transfers between devices  7.37 us (20%)
  waiting for transfers between devices  1.89 us (5%)
  local copies, waits for them, and re-layouts  1.69 us (5%)
    all_to_all x1, blocking collectives, exchange(): lax.all_to_all(parts, 'row', split_axis=0, concat_axis=0, tiled=True, axi...  14.9 us
    all_to_all x1, starting transfers between devices, exchange(): lax.all_to_all(parts, 'row', split_axis=0, concat_axis=0, tiled=True, axi...  7.37 us
    pallas_call x1, Pallas kernels, local(): pl.pallas_call(bias_kernel, grid=(1,), out_shape=shape((parties, bias_row...  3.25 us
    pallas_call x1, Pallas kernels, local(): pl.pallas_call(functools.partial(second_kernel, rows, rank), grid=(1,), o...  3.23 us
    pallas_call x1, Pallas kernels, local(): pl.pallas_call(functools.partial(first_kernel, rank), grid=(1,), out_shap...  1.97 us
    all_to_all x1, waiting for transfers between devices, exchange(): lax.all_to_all(parts, 'row', split_axis=0, concat_axis=0, tiled=True, axi...  1.89 us
    unnamed x18, local copies, waits for them, and re-layouts  1.69 us
    pallas_call x1, Pallas kernels, local(): pl.pallas_call(functools.partial(project_kernel, heads), grid=(1,), out_s...  1.54 us
  transfers between devices with their start and end apart: 1, of which 1 were waited for; matrix products, arithmetic and copies ran while one was open for 0% of the time, Pallas kernels for 4%

profile of v3, /device:TPU:1, one launch (start us, length us, event | category | flops | bytes accessed | tf_op | source)
XLA Modules:
  0.0 35.9 jit_solution(15024352739052356456)
XLA Ops:
  0.0 0.0 copy-start.4
  0.0 0.0 copy-start.6
  0.0 0.0 copy-start.7
  0.0 3.2 %bias.1 = bf16[16,32,128]{2,1,0:T(8,128)(2,1)} custom-call(f32[8,128,128]{2,1,0:T(8,128)} %x_ref.5, f32[2,128]{1,0:T(2,128)} %gain_ref.7, bf16[2,4,128]{2,1,0:T(4,128)(2,1)} %bitcast.3), custom_call_target="tpu_custom_call" | custom-call | tf_op jit(solution)/shard_map/bias/pallas_call | solution.py:294
  3.3 0.0 copy-start.2
  3.3 7.4 %all-to-all-start = ((bf16[16,32,128]{2,1,0:T(8,128)(2,1)}), bf16[16,32,128]{2,1,0:T(8,128)(2,1)S(1)}, u32[]{:S(2)}, u32[]{:S(2)}) async-start(bf16[16,32,128]{2,1,0:T(8,128)(2,1)} %bias.1), calls=%async_computation | async-start | bytes 262144 | tf_op jit(solution)/shard_map/all_to_all | solution.py:291
  10.7 0.0 copy-start.5
  10.7 0.0 copy-start.8
  10.7 0.0 copy-done.4
  10.7 0.0 copy-done.6
  10.7 0.0 copy-done.7
  10.7 0.0 copy-done.2
  10.7 0.6 %copy-done.5 = f32[2,128]{1,0:T(2,128)S(1)} copy-done((f32[2,128]{1,0:T(2,128)S(1)}, f32[2,128]{1,0:T(2,128)}, u32[]{:S(2)}) %copy-start.5) | copy-done | bytes 1048
  11.3 0.0 copy-done.8
  11.3 0.0 copy-start
  11.3 1.0 %copy-done = f32[8,128,128]{2,1,0:T(8,128)S(1)} copy-done((f32[8,128,128]{2,1,0:T(8,128)S(1)}, f32[8,128,128]{2,1,0:T(8,128)}, u32[]{:S(2)}) %copy-start) | copy-done | bytes 524312
  12.4 0.0 copy-start.1
  12.4 0.0 copy-start.3
  12.4 1.5 %project.1 = (bf16[8,128,128]{2,1,0:T(8,128)(2,1)S(1)}, bf16[8,128,128]{2,1,0:T(8,128)(2,1)S(1)}, bf16[8,128,128]{2,1,0:T(8,128)(2,1)S(1)}, f32[8,128,128]{2,1,0:T(8,128)S(1)}, s32[8,128]{1,0:T(8,128)S(1)}) custom-call(f32[8,128,128]{2,1,0:T(8,128)S(1)} %copy-done, f32[2,128]{1,0:T(2,128)S(1)} %copy-done.5, s32[128]{0:T(128)S(1)} %copy-done.8, ...), custom_call_target="tpu_custom_call" | custom-call | flops 134217728 | bytes 1572864 | tf_op jit(solution)/shard_map/project/pallas_call | solution.py:311
  13.9 1.9 %all-to-all-done.got_ref = bf16[16,32,128]{2,1,0:T(8,128)(2,1)S(1)} async-done(((bf16[16,32,128]{2,1,0:T(8,128)(2,1)}), bf16[16,32,128]{2,1,0:T(8,128)(2,1)S(1)}, u32[]{:S(2)}, u32[]{:S(2)}) %all-to-all-start) | async-done | bytes 131104 | tf_op jit(solution)/shard_map/all_to_all | solution.py:291
  15.8 0.0 copy-done.1
  15.8 0.0 copy-done.3
  15.8 2.0 %first.1 = bf16[16,96,128]{2,1,0:T(8,128)(2,1)S(1)} custom-call(f32[8,128,128]{2,1,0:T(8,128)S(1)} %copy-done.1, bf16[8,128,128]{2,1,0:T(8,128)(2,1)S(1)} %get-tuple-element.10.q_ref, bf16[8,128,128]{2,1,0:T(8,128)(2,1)S(1)} %get-tuple-element.11.k_ref, bf16[8,128,128]{2,1,0:T(8,128)(2,1)S(1)} %get-tuple-element.12.v_ref, ...), custom_call_target="tpu_custom_call" | custom-call | tf_op jit(solution)/shard_map/first/pallas_call | solution.py:332
  17.8 14.9 %all_to_all.10.got_ref = bf16[16,96,128]{2,1,0:T(8,128)(2,1)S(1)} all-to-all(bf16[16,96,128]{2,1,0:T(8,128)(2,1)S(1)} %first.1), channel_id=1, replica_groups={{9,8,4,12,0,5,13,1,10,6,14,2,11,7,15,3},{25,24,20,28,16,21,29,17,26,22,..., dimensions={0} | all-to-all | bytes 786432 | tf_op jit(solution)/shard_map/all_to_all | solution.py:291
  32.7 3.2 %second.1 = f32[1024,128]{1,0:T(8,128)} custom-call(bf16[16,96,128]{2,1,0:T(8,128)(2,1)S(1)} %all_to_all.10.got_ref, s32[8,128]{1,0:T(8,128)S(1)} %get-tuple-element.14.keep_ref, f32[2,128]{1,0:T(2,128)S(1)} %copy-done.5, bf16[2,128,512]{2,1,0:T(8,128)(2,1)S(1)} %copy-done.2, f32[2,128]{1,0:T(2,128)S(1)} %copy-done.7, bf16[2,128,128]{2,1,0:T(8,128)(2,1)S(1)} %copy-done.3, ...), custom_call_target="tpu_custom_call" | custom-call | tf_op jit(solution)/shard_map/second/pallas_call | solution.py:346
Async XLA Ops:
  0.0 10.7 %copy-start.4 = (bf16[2,128,4]{1,2,0:T(4,128)(2,1)S(1)}, bf16[2,128,4]{1,2,0:T(4,128)(2,1)}, u32[]{:S(2)}) copy-start(bf16[2,128,4]{1,2,0:T(4,128)(2,1)} %param.12) | copy-start | bytes 6148
  0.0 10.7 %copy-start.6 = (f32[2,128]{1,0:T(2,128)S(1)}, f32[2,128]{1,0:T(2,128)}, u32[]{:S(2)}) copy-start(f32[2,128]{1,0:T(2,128)} %out_bias_ref.3) | copy-start | bytes 3076
  0.0 10.7 %copy-start.7 = (f32[2,128]{1,0:T(2,128)S(1)}, f32[2,128]{1,0:T(2,128)}, u32[]{:S(2)}) copy-start(f32[2,128]{1,0:T(2,128)} %gate_bias_ref.3) | copy-start | bytes 3076
  3.3 7.4 %copy-start.2 = (bf16[2,128,512]{2,1,0:T(8,128)(2,1)S(1)}, bf16[2,128,512]{2,1,0:T(8,128)(2,1)}, u32[]{:S(2)}) copy-start(bf16[2,128,512]{2,1,0:T(8,128)(2,1)} %w_ref.3) | copy-start | bytes 786436
  3.3 12.5 %all-to-all-start = ((bf16[16,32,128]{2,1,0:T(8,128)(2,1)}), bf16[16,32,128]{2,1,0:T(8,128)(2,1)S(1)}, u32[]{:S(2)}, u32[]{:S(2)}) async-start(bf16[16,32,128]{2,1,0:T(8,128)(2,1)} %bias.1), calls=%async_computation | async-start | bytes 262144 | tf_op jit(solution)/shard_map/all_to_all | solution.py:291
  10.7 0.7 %copy-start.5 = (f32[2,128]{1,0:T(2,128)S(1)}, f32[2,128]{1,0:T(2,128)}, u32[]{:S(2)}) copy-start(f32[2,128]{1,0:T(2,128)} %gain_ref.7) | copy-start | bytes 3076
  10.7 0.7 %copy-start.8 = (s32[128]{0:T(128)S(1)}, s32[128]{0:T(128)}, u32[]{:S(2)}) copy-start(s32[128]{0:T(128)} %flag_ref.1) | copy-start | bytes 1540
  11.3 1.0 %copy-start = (f32[8,128,128]{2,1,0:T(8,128)S(1)}, f32[8,128,128]{2,1,0:T(8,128)}, u32[]{:S(2)}) copy-start(f32[8,128,128]{2,1,0:T(8,128)} %x_ref.5) | copy-start | bytes 1572868
  12.4 3.4 %copy-start.1 = (f32[8,128,128]{2,1,0:T(8,128)S(1)}, f32[8,128,128]{2,1,0:T(8,128)}, u32[]{:S(2)}) copy-start(f32[8,128,128]{2,1,0:T(8,128)} %x_ref.5) | copy-start | bytes 1572868
  12.4 3.4 %copy-start.3 = (bf16[2,128,128]{2,1,0:T(8,128)(2,1)S(1)}, bf16[2,128,128]{2,1,0:T(8,128)(2,1)}, u32[]{:S(2)}) copy-start(bf16[2,128,128]{2,1,0:T(8,128)(2,1)} %w_out_ref.3) | copy-start | bytes 196612

commit v4 on v3

v4 whole, which is shorter than its diff:
```python
import functools

import jax
import jax.numpy as jnp
from jax import lax
from jax.experimental import pallas as pl
from jax.experimental.pallas import tpu as pltpu
from jax.sharding import PartitionSpec as P

LANES = 128
VMEM_BYTES = 24 * 2**20
KEPT = 2
PIECE = 32
TOKENS = 1024
F32 = jnp.float32
BF16 = jnp.bfloat16
MASKED = -1000000000.0
EPSILON = 1e-05
LOG2E = 1.4426950408889634


def dot(a, b, dims=((1,), (0,))):
    return lax.dot_general(a, b, (dims, ((), ())), preferred_element_type=F32)


def in_step(streams, together):
    streams = list(streams)
    for at in range(0, len(streams), together):
        group = streams[at : at + together]
        while group:
            group = [stream for stream in group if next(stream, group) is not group]


def own_rows(turned, h, heads):
    width, n = turned.shape
    dim = width // heads
    parts = [turned[h * dim : (h + 1) * dim]]
    if h:
        parts.insert(0, jnp.zeros((h * dim, n), turned.dtype))
    if h < heads - 1:
        parts.append(jnp.zeros((width - (h + 1) * dim, n), turned.dtype))
    return jnp.concatenate(parts, axis=0)


def query_block(qt, picked, heads):
    return jnp.concatenate([own_rows(qt, h, heads) for h in picked], axis=1)


def attention(k, qt, vt, gt, bias, lift, heads, result):
    dim = vt.shape[0] // heads
    weights = []
    for picked in pairs_of(heads):
        scores = dot(k, query_block(qt, picked, heads))
        for n, h in enumerate(picked):
            part = scores[:, n * LANES : (n + 1) * LANES] + bias(h)
            part = jnp.exp2(part - jnp.max(part, axis=0, keepdims=True)).astype(BF16)
            weights.append(jnp.maximum(part, lift))
            yield
    ones = jnp.ones((16, vt.shape[1]), BF16)
    mixture = []
    for picked in pairs_of(heads):
        rows = jnp.concatenate([vt[h * dim : (h + 1) * dim] for h in picked] + [ones], axis=0)
        both = dot(rows, jnp.concatenate([weights[h] for h in picked], axis=1))
        for n, h in enumerate(picked):
            column = both[:, n * LANES : (n + 1) * LANES]
            mixture.append(column[n * dim : (n + 1) * dim] * (1.0 / column[len(picked) * dim : len(picked) * dim + 1]))
        yield
    result.append((gt * jnp.concatenate(mixture, axis=0)).astype(BF16))


def turned_weights(w, width):
    sides = [w[:, at * width : (at + 1) * width] for at in (0, 2, 3)]
    return jnp.concatenate([side.T for side in sides], axis=0), w[:, width : 2 * width]


def gate_column(row, length):
    column = jnp.broadcast_to(row, (LANES, row.shape[1])).T
    return jnp.concatenate([column] * (length // LANES), axis=1)


def lift_of(row, length):
    return jnp.broadcast_to(row, (length, LANES)).astype(BF16)


def masked(part, column):
    return jnp.where(column > 0, part * LOG2E, F32(MASKED))


def projected(x, sides, keys, gate, scaling):
    width = keys.shape[1]
    three = dot(sides, x, ((1,), (1,)))
    qt = (three[:width] * scaling).astype(BF16)
    vt = three[width : 2 * width].astype(BF16)
    gt = jax.nn.sigmoid(three[2 * width :] + gate)
    return qt, dot(x, keys).astype(BF16), vt, gt


def pairs_of(heads):
    return [tuple(range(h, min(h + 2, heads))) for h in range(0, heads, 2)]


def bias_kernel(x_ref, gain_ref, w_tri_ref, send_ref, rows_ref, held_ref, scale_ref, weight_ref, sems):
    rows, length, _ = x_ref.shape
    heads = w_tri_ref.shape[1]
    copies = [
        pltpu.make_async_copy(x_ref, held_ref, sems.at[0]),
        pltpu.make_async_copy(gain_ref, scale_ref, sems.at[1]),
        pltpu.make_async_copy(w_tri_ref.at[0], weight_ref, sems.at[2]),
    ]
    for copy in copies:
        copy.start()
    for copy in copies:
        copy.wait()

    scale = scale_ref[0:1, :] * held_ref.shape[2] ** 0.5

    def stream(i, t):
        x = held_ref[i, t * LANES : (t + 1) * LANES, :]
        shifted = x - jnp.mean(x, axis=-1, keepdims=True)
        yield
        spread = jnp.sum(shifted * shifted, axis=-1, keepdims=True)
        yield
        x = (shifted * lax.rsqrt(spread + EPSILON * x.shape[1]) * scale).astype(BF16)
        yield
        rows_ref[pl.ds(t * heads * rows + i, heads, stride=rows), :] = dot(weight_ref[...], x, ((1,), (1,)))

    in_step((stream(i, t) for i in range(rows) for t in range(length // LANES)), max(TOKENS // length, 1))
    packed = rows_ref[...].astype(BF16)
    for d in range(send_ref.shape[0]):
        send_ref[d] = packed


def project_kernel(heads, x_ref, gain_ref, flag_ref, mask_ref, w_ref, gate_bias_ref, *more_refs):
    q_ref, k_ref, v_ref, g_ref, column_ref, lift_ref = more_refs[KEPT:]
    rows, length, width = k_ref.shape
    scaling = (width // heads) ** (-0.5) * LOG2E
    sides, keys = turned_weights(w_ref[0], width)
    gate = gate_column(gate_bias_ref[0:1, :], length)
    first = lax.axis_index("row") * rows
    for i in range(rows):
        lift_ref[i : i + 1, :] = jnp.full((1, LANES), jnp.where(flag_ref[first + i] > 0, F32(0.0), F32(1.0)))
    column_ref[...] = jnp.broadcast_to((mask_ref[...] > 0).astype(F32), (LANES, length)).T
    gain = gain_ref[0:1, :] * x_ref.shape[2] ** 0.5

    def stream(i):
        x = x_ref[i]
        shifted = x - jnp.mean(x, axis=-1, keepdims=True)
        yield
        spread = jnp.sum(shifted * shifted, axis=-1, keepdims=True)
        yield
        x = (shifted * lax.rsqrt(spread + EPSILON * x.shape[1]) * gain).astype(BF16)
        q_ref[i], k_ref[i], v_ref[i], g_ref[i] = projected(x, sides, keys, gate, scaling)

    in_step((stream(i) for i in range(rows)), max(TOKENS // length, 1))


def first_kernel(
    rank, rank_out, x_ref, q_ref, k_ref, v_ref, g_ref, got_ref, column_ref, lift_ref, gain_ref, w_tri_ref, w_out_ref,
    out_bias_ref, send_ref, bias_ref, rows_ref,
):
    rows, length, width = k_ref.shape
    heads = w_tri_ref.shape[1]
    parties = send_ref.shape[0]
    share = length // parties
    blocks = length // LANES
    reach = LANES // share
    for h in range(heads):
        for t in range(blocks):
            at = (t * heads + h) * rows
            for b in range(blocks):
                part = jnp.concatenate(
                    [got_ref[rank[s], at : at + rows, :].astype(F32) for s in range(b * reach, (b + 1) * reach)], axis=0
                )
                span = slice(t * LANES, (t + 1) * LANES)
                bias_ref[span, (b * heads + h) * LANES : (b * heads + h + 1) * LANES] = masked(
                    part.T, column_ref[span, :]
                )
    gain = gain_ref[1:2, :] * x_ref.shape[2] ** 0.5

    def stream(i, t):
        span = slice(t * LANES, (t + 1) * LANES)
        lift = lift_of(lift_ref[i : i + 1, :], length)
        result = []

        def bias(h):
            return bias_ref[:, (t * heads + h) * LANES : (t * heads + h + 1) * LANES]

        yield from attention(
            k_ref[i], q_ref[i, :, span], v_ref[i], g_ref[i, :, span], bias, lift, heads, result
        )
        stacked = x_ref[i, span, :] + (dot(result[0], w_out_ref[0], ((0,), (0,))) + out_bias_ref[0:1, :])
        for d in range(reach):
            send_ref[rank_out[t * reach + d], i * share : (i + 1) * share, :] = stacked[
                d * share : (d + 1) * share
            ].astype(BF16)
        yield
        shifted = stacked - jnp.mean(stacked, axis=-1, keepdims=True)
        yield
        spread = jnp.sum(shifted * shifted, axis=-1, keepdims=True)
        yield
        x = (shifted * lax.rsqrt(spread + EPSILON * stacked.shape[1]) * gain).astype(BF16)
        rows_ref[pl.ds(t * heads * rows + i, heads, stride=rows), :] = dot(w_tri_ref[0], x, ((1,), (1,)))

    in_step((stream(i, t) for i in range(rows) for t in range(blocks)), max(TOKENS // length, 1))
    packed = rows_ref[...].astype(BF16)
    for d in range(parties):
        send_ref[d, rows * share :, :] = packed


def second_kernel(
    rows, rank, got_ref, column_ref, lift_ref, gain_ref, w_ref, gate_bias_ref, w_out_ref, out_bias_ref,
    out_ref, held_ref, bias_ref, sems,
):
    parties = got_ref.shape[0]
    length = column_ref.shape[0]
    share = length // parties
    blocks = length // LANES
    width = w_ref.shape[2] // 4
    heads = bias_ref.shape[1] // length
    scaling = (width // heads) ** (-0.5) * LOG2E
    for s in range(parties):
        held_ref[s * rows * share : (s + 1) * rows * share, :] = got_ref[rank[s], : rows * share, :].astype(F32)
    for n in range(heads * blocks):
        at = rows * share + n * rows
        for s in range(parties):
            span = slice(s * rows, (s + 1) * rows)
            bias_ref[span, n * LANES : (n + 1) * LANES] = masked(
                got_ref[rank[s], at : at + rows, :].astype(F32), column_ref[span, :]
            )
    sides, keys = turned_weights(w_ref[0], width)
    gate = gate_column(gate_bias_ref[1:2, :], length)
    gain = gain_ref[1:2, :] * held_ref.shape[1] ** 0.5

    def piece(n):
        at = pl.ds(n * PIECE * share, PIECE * share)
        return pltpu.make_async_copy(held_ref.at[at], out_ref.at[at], sems.at[n])

    copies = [piece(n) for n in range(length // PIECE)]
    stored = [0] * len(copies)
    sent = [0]

    def stream(j):
        x = held_ref[pl.ds(j, length, stride=share), :]
        shifted = x - jnp.mean(x, axis=-1, keepdims=True)
        yield
        spread = jnp.sum(shifted * shifted, axis=-1, keepdims=True)
        yield
        x = (shifted * lax.rsqrt(spread + EPSILON * x.shape[1]) * gain).astype(BF16)
        qt, k, vt, gt = projected(x, sides, keys, gate, scaling)
        yield
        lift = lift_of(lift_ref[j : j + 1, :], length)
        for t in range(blocks):
            span = slice(t * LANES, (t + 1) * LANES)
            result = []

            def bias(h, t=t):
                return bias_ref[:, (t * heads + h) * LANES : (t * heads + h + 1) * LANES]

            yield from attention(k, qt[:, span], vt, gt[:, span], bias, lift, heads, result)
            update = dot(result[0], w_out_ref[0], ((0,), (0,))) + out_bias_ref[1:2, :]
            yield
            for p in range(LANES // PIECE):
                at = pl.ds((t * LANES + p * PIECE) * share + j, PIECE, stride=share)
                held_ref[at, :] = held_ref[at, :] + update[p * PIECE : (p + 1) * PIECE]
                stored[t * (LANES // PIECE) + p] += 1
                while sent[0] < len(copies) and stored[min(sent[0] + 1, len(copies) - 1)] == share:
                    copies[sent[0]].start()
                    sent[0] += 1
                yield

    in_step((stream(j) for j in range(share)), max(TOKENS // length, 1))
    for copy in copies:
        copy.wait()


def of_pass(array, p):
    shape = (1,) + array.shape[1:]
    return pl.BlockSpec(shape, lambda *_: (p,) + (0,) * (len(shape) - 1))


SMEM = pl.BlockSpec(memory_space=pltpu.SMEM)


def group_order(parties, lead):
    stride = max(parties // 4, 1)
    order = [m * stride + k for k in range(stride) for m in (2, 1, 3, 0) if m * stride + k < parties]
    return [lead] + [d for d in order if d != lead]


def params(limit=VMEM_BYTES):
    return pltpu.CompilerParams(vmem_limit_bytes=limit)


def local(parties, pair_rep, token_mask, ln_gain, w_proj, w_tri, gate_bias, w_out, out_bias):
    rows, length, channels = pair_rep.shape
    heads = w_tri.shape[2]
    width = w_proj.shape[2] // 4
    share = length // parties
    bias_rows = length // LANES * heads * rows
    mask = token_mask.reshape(1, length)
    w_tri = jnp.swapaxes(w_tri, 1, 2)
    shape = jax.ShapeDtypeStruct

    def full(array):
        return pl.BlockSpec(array.shape, lambda *_: (0,) * array.ndim)

    middle = parties // 2
    early = group_order(parties, (middle + 3) % parties)
    late = group_order(parties, (middle + 1) % parties)

    def ranks(order):
        return [order.index(d) for d in range(parties)]

    def exchange(parts, order):
        return lax.all_to_all(parts, "row", split_axis=0, concat_axis=0, tiled=True, axis_index_groups=[order])

    hbm = pl.BlockSpec(memory_space=pltpu.HBM)
    send = pl.pallas_call(
        bias_kernel,
        grid=(1,),
        out_shape=shape((parties, bias_rows, LANES), BF16),
        in_specs=[hbm, hbm, hbm],
        scratch_shapes=[
            pltpu.VMEM((bias_rows, LANES), F32),
            pltpu.VMEM(pair_rep.shape, F32),
            pltpu.VMEM(ln_gain.shape, F32),
            pltpu.VMEM(w_tri.shape[1:], BF16),
            pltpu.SemaphoreType.DMA((3,)),
        ],
        compiler_params=params(),
        name="bias",
    )(*(pltpu.with_memory_space_constraint(a, pltpu.HBM) for a in (pair_rep, ln_gain, w_tri)))
    got = exchange(send, early)
    kept = (w_tri, out_bias)
    q, k, v, g, column, lift = pl.pallas_call(
        functools.partial(project_kernel, heads),
        grid=(1,),
        out_shape=(
            shape((rows, width, length), BF16),
            shape((rows, length, width), BF16),
            shape((rows, width, length), BF16),
            shape((rows, width, length), F32),
            shape((length, LANES), F32),
            shape((rows, LANES), F32),
        ),
        in_specs=[full(pair_rep), full(ln_gain), SMEM, full(mask), of_pass(w_proj, 0), full(gate_bias)]
        + [full(a) for a in kept],
        compiler_params=params(),
        cost_estimate=pl.CostEstimate(
            flops=2 * rows * length * channels * 4 * width,
            transcendentals=rows * length * width,
            bytes_accessed=rows * length * width * 12,
        ),
        name="project",
    )(pair_rep, ln_gain, token_mask, mask, w_proj, gate_bias, *kept)
    taken = (pair_rep, q, k, v, g, got, column, lift, ln_gain)
    send = pl.pallas_call(
        functools.partial(first_kernel, ranks(early), ranks(late)),
        grid=(1,),
        out_shape=shape((parties, rows * share + bias_rows, LANES), BF16),
        in_specs=[full(a) for a in taken]
        + [of_pass(w_tri, 1), of_pass(w_out, 0), full(out_bias)],
        scratch_shapes=[
            pltpu.VMEM((length, heads * length), F32),
            pltpu.VMEM((bias_rows, LANES), F32),
        ],
        compiler_params=params(),
        name="first",
    )(*taken, w_tri, w_out, out_bias)
    got = exchange(send, late)
    out = pl.pallas_call(
        functools.partial(second_kernel, rows, ranks(late)),
        grid=(1,),
        out_shape=shape((length * share, channels), F32),
        in_specs=[
            full(got), full(column), full(lift), full(ln_gain), of_pass(w_proj, 1), full(gate_bias), of_pass(w_out, 1),
            full(out_bias),
        ],
        out_specs=hbm,
        scratch_shapes=[
            pltpu.VMEM((length * share, channels), F32),
            pltpu.VMEM((length, heads * length), F32),
            pltpu.SemaphoreType.DMA((length // PIECE,)),
        ],
        compiler_params=params(),
        name="second",
    )(got, column, lift, ln_gain, w_proj, gate_bias, w_out, out_bias)
    return out.reshape(length, share, channels)


def solution(mesh):
    return jax.shard_map(
        functools.partial(local, mesh.shape["row"]),
        mesh=mesh,
        in_specs=(P(("group", "row"), None, None), P("group"), P(), P(), P(), P(), P(), P()),
        out_specs=P("group", "row", None),
        check_vma=False,
    )
```

time: 36.3 us -> 34.1 us (0.939)
  Pallas kernels: 9.99 us -> 7.77 us
  local copies, waits for them, and re-layouts: 1.69 us -> 0.64 us
  blocking collectives: 14.9 us -> 15.4 us
  waiting for transfers between devices: 1.89 us -> 2.27 us
    pallas_call x2, Pallas kernels: 5.2 us -> 3.98 us  [the longest x1 2.56 us: local(): pl.pallas_call(functools.partial(second_kernel, rows, ranks(late)), grid=...]
    unnamed x18 -> x16, local copies, waits for them, and re-layouts: 1.69 us -> 0.64 us
    pallas_call x1, Pallas kernels: 3.25 us -> 2.32 us  [local(): pl.pallas_call(bias_kernel, grid=(1,), out_shape=shape((parties, bias_row...]
    all_to_all x1, blocking collectives: 14.9 us -> 15.4 us  [exchange(): lax.all_to_all(parts, 'row', split_axis=0, concat_axis=0, tiled=True, axi...]
    all_to_all x1, waiting for transfers between devices: 1.89 us -> 2.27 us  [exchange(): lax.all_to_all(parts, 'row', split_axis=0, concat_axis=0, tiled=True, axi...]
where the time goes in v4:
time: 34.1 us; the launch traced here: 33.8 us
  blocking collectives  15.4 us (45%)
  Pallas kernels  7.77 us (23%)
  starting transfers between devices  7.57 us (22%)
  waiting for transfers between devices  2.27 us (7%)
  local copies, waits for them, and re-layouts  0.64 us (2%)
    all_to_all x1, blocking collectives, exchange(): lax.all_to_all(parts, 'row', split_axis=0, concat_axis=0, tiled=True, axi...  15.4 us
    all_to_all x1, starting transfers between devices, exchange(): lax.all_to_all(parts, 'row', split_axis=0, concat_axis=0, tiled=True, axi...  7.57 us
    pallas_call x1, Pallas kernels, local(): pl.pallas_call(functools.partial(second_kernel, rows, ranks(late)), grid=...  2.56 us
    pallas_call x1, Pallas kernels, local(): pl.pallas_call(bias_kernel, grid=(1,), out_shape=shape((parties, bias_row...  2.32 us
    all_to_all x1, waiting for transfers between devices, exchange(): lax.all_to_all(parts, 'row', split_axis=0, concat_axis=0, tiled=True, axi...  2.27 us
    pallas_call x1, Pallas kernels, local(): pl.pallas_call(functools.partial(project_kernel, heads), grid=(1,), out_s...  1.47 us
    pallas_call x1, Pallas kernels, local(): pl.pallas_call(functools.partial(first_kernel, ranks(early), ranks(late))...  1.42 us
  transfers between devices with their start and end apart: 1, of which 1 were waited for; matrix products, arithmetic and copies ran while one was open for 0% of the time, Pallas kernels for 4%

profile of v4, /device:TPU:1, one launch (start us, length us, event | category | flops | bytes accessed | tf_op | source)
XLA Modules:
  0.0 33.8 jit_solution(1890588223213944681)
XLA Ops:
  0.0 0.0 copy-start
  0.0 0.0 copy-start.3
  0.0 0.0 copy-start.5
  0.0 0.0 copy-start.6
  0.0 2.3 %bias.1 = bf16[16,32,128]{2,1,0:T(8,128)(2,1)} custom-call(f32[8,128,128]{2,1,0:T(8,128)} %x_ref.5, f32[2,128]{1,0:T(2,128)} %gain_ref.7, bf16[2,4,128]{2,1,0:T(4,128)(2,1)} %bitcast.3), custom_call_target="tpu_custom_call" | custom-call | tf_op jit(solution)/shard_map/bias/pallas_call | solution.py:318
  2.3 0.0 copy-start.1
  2.4 7.6 %all-to-all-start = ((bf16[16,32,128]{2,1,0:T(8,128)(2,1)}), bf16[16,32,128]{2,1,0:T(8,128)(2,1)S(1)}, u32[]{:S(2)}, u32[]{:S(2)}) async-start(bf16[16,32,128]{2,1,0:T(8,128)(2,1)} %bias.1), calls=%async_computation | async-start | bytes 262144 | tf_op jit(solution)/shard_map/all_to_all | solution.py:315
  9.9 0.0 copy-start.4
  9.9 0.0 copy-start.7
  10.0 0.0 copy-done
  10.0 0.0 copy-done.3
  10.0 0.0 copy-done.5
  10.0 0.0 copy-done.6
  10.0 0.0 copy-done.1
  10.0 0.6 %copy-done.4 = f32[2,128]{1,0:T(2,128)S(1)} copy-done((f32[2,128]{1,0:T(2,128)S(1)}, f32[2,128]{1,0:T(2,128)}, u32[]{:S(2)}) %copy-start.4) | copy-done | bytes 1048
  10.6 0.0 copy-done.7
  10.6 0.0 copy-start.2
  10.6 1.5 %project.1 = (bf16[8,128,128]{2,1,0:T(8,128)(2,1)S(1)}, bf16[8,128,128]{2,1,0:T(8,128)(2,1)S(1)}, bf16[8,128,128]{2,1,0:T(8,128)(2,1)S(1)}, f32[8,128,128]{2,1,0...) custom-call(f32[8,128,128]{2,1,0:T(8,128)S(1)} %copy-done, f32[2,128]{1,0:T(2,128)S(1)} %copy-done.4, ...), custom_call_target="tpu_custom_call" | custom-call | flops 134217728 | bytes 1572864 | tf_op jit(solution)/shard_map/project/pallas_call | solution.py:335
  12.1 2.3 %all-to-all-done.got_ref = bf16[16,32,128]{2,1,0:T(8,128)(2,1)S(1)} async-done(((bf16[16,32,128]{2,1,0:T(8,128)(2,1)}), bf16[16,32,128]{2,1,0:T(8,128)(2,1)S(1)}, u32[]{:S(2)}, u32[]{:S(2)}) %all-to-all-start) | async-done | bytes 131104 | tf_op jit(solution)/shard_map/all_to_all | solution.py:315
  14.4 0.0 copy-done.2
  14.4 1.4 %first.1 = bf16[16,96,128]{2,1,0:T(8,128)(2,1)S(1)} custom-call(f32[8,128,128]{2,1,0:T(8,128)S(1)} %copy-done, bf16[8,128,128]{2,1,0:T(8,128)(2,1)S(1)} %get-tuple-element.11.q_ref, bf16[8,128,128]{2,1,0:T(8,128)(2,1)S(1)} %get-tuple-element.12.k_ref, bf16[8,128,128]{2,1,0:T(8,128)(2,1)S(1)} %get-tuple-element.13.v_ref, ...), custom_call_target="tpu_custom_call" | custom-call | tf_op jit(solution)/shard_map/first/pallas_call | solution.py:357
  15.8 15.4 %all_to_all.10.got_ref = bf16[16,96,128]{2,1,0:T(8,128)(2,1)S(1)} all-to-all(bf16[16,96,128]{2,1,0:T(8,128)(2,1)S(1)} %first.1), channel_id=1, replica_groups={{9,8,4,12,0,5,13,1,10,6,14,2,11,7,15,3},{25,24,20,28,16,21,29,17,26,22,..., dimensions={0} | all-to-all | bytes 786432 | tf_op jit(solution)/shard_map/all_to_all | solution.py:315
  31.2 2.6 %second.1 = f32[1024,128]{1,0:T(8,128)} custom-call(bf16[16,96,128]{2,1,0:T(8,128)(2,1)S(1)} %all_to_all.10.got_ref, f32[128,128]{1,0:T(8,128)S(1)} %get-tuple-element.15.column_ref, f32[8,128]{1,0:T(8,128)S(1)} %get-tuple-element.16.lift_ref, f32[2,128]{1,0:T(2,128)S(1)} %copy-done.4, bf16[2,128,512]{2,1,0:T(8,128)(2,1)S(1)} %copy-done.1, ...), custom_call_target="tpu_custom_call" | custom-call | tf_op jit(solution)/shard_map/second/pallas_call | solution.py:371
Async XLA Ops:
  0.0 10.0 %copy-start = (f32[8,128,128]{2,1,0:T(8,128)S(1)}, f32[8,128,128]{2,1,0:T(8,128)}, u32[]{:S(2)}) copy-start(f32[8,128,128]{2,1,0:T(8,128)} %x_ref.5) | copy-start | bytes 1572868
  0.0 10.0 %copy-start.3 = (bf16[2,128,4]{1,2,0:T(4,128)(2,1)S(1)}, bf16[2,128,4]{1,2,0:T(4,128)(2,1)}, u32[]{:S(2)}) copy-start(bf16[2,128,4]{1,2,0:T(4,128)(2,1)} %param.12) | copy-start | bytes 6148
  0.0 10.0 %copy-start.5 = (f32[2,128]{1,0:T(2,128)S(1)}, f32[2,128]{1,0:T(2,128)}, u32[]{:S(2)}) copy-start(f32[2,128]{1,0:T(2,128)} %out_bias_ref.3) | copy-start | bytes 3076
  0.0 10.0 %copy-start.6 = (f32[2,128]{1,0:T(2,128)S(1)}, f32[2,128]{1,0:T(2,128)}, u32[]{:S(2)}) copy-start(f32[2,128]{1,0:T(2,128)} %gate_bias_ref.3) | copy-start | bytes 3076
  2.3 7.6 %copy-start.1 = (bf16[2,128,512]{2,1,0:T(8,128)(2,1)S(1)}, bf16[2,128,512]{2,1,0:T(8,128)(2,1)}, u32[]{:S(2)}) copy-start(bf16[2,128,512]{2,1,0:T(8,128)(2,1)} %w_ref.3) | copy-start | bytes 786436
  2.4 12.0 %all-to-all-start = ((bf16[16,32,128]{2,1,0:T(8,128)(2,1)}), bf16[16,32,128]{2,1,0:T(8,128)(2,1)S(1)}, u32[]{:S(2)}, u32[]{:S(2)}) async-start(bf16[16,32,128]{2,1,0:T(8,128)(2,1)} %bias.1), calls=%async_computation | async-start | bytes 262144 | tf_op jit(solution)/shard_map/all_to_all | solution.py:315
  9.9 0.7 %copy-start.4 = (f32[2,128]{1,0:T(2,128)S(1)}, f32[2,128]{1,0:T(2,128)}, u32[]{:S(2)}) copy-start(f32[2,128]{1,0:T(2,128)} %gain_ref.7) | copy-start | bytes 3076
  9.9 0.7 %copy-start.7 = (s32[128]{0:T(128)S(1)}, s32[128]{0:T(128)}, u32[]{:S(2)}) copy-start(s32[128]{0:T(128)} %flag_ref.1) | copy-start | bytes 1540
  10.6 3.7 %copy-start.2 = (bf16[2,128,128]{2,1,0:T(8,128)(2,1)S(1)}, bf16[2,128,128]{2,1,0:T(8,128)(2,1)}, u32[]{:S(2)}) copy-start(bf16[2,128,128]{2,1,0:T(8,128)(2,1)} %w_out_ref.3) | copy-start | bytes 196612

commit v5 on v4

--- a/solution.py
+++ b/solution.py
@@ -29,6 +29,13 @@
         group = streams[at : at + together]
         while group:
             group = [stream for stream in group if next(stream, group) is not group]
+
+
+def row_sums(x):
+    ones = jnp.ones((x.shape[1], x.shape[1]), BF16)
+    upper = x.astype(BF16)
+    lower = (x - upper.astype(F32)).astype(BF16)
+    return dot(upper, ones) + dot(lower, ones)
 
 
 def own_rows(turned, h, heads):
@@ -118,7 +125,7 @@
         x = held_ref[i, t * LANES : (t + 1) * LANES, :]
         shifted = x - jnp.mean(x, axis=-1, keepdims=True)
         yield
-        spread = jnp.sum(shifted * shifted, axis=-1, keepdims=True)
+        spread = row_sums(shifted * shifted)
         yield
         x = (shifted * lax.rsqrt(spread + EPSILON * x.shape[1]) * scale).astype(BF16)
         yield
@@ -146,7 +153,7 @@
         x = x_ref[i]
         shifted = x - jnp.mean(x, axis=-1, keepdims=True)
         yield
-        spread = jnp.sum(shifted * shifted, axis=-1, keepdims=True)
+        spread = row_sums(shifted * shifted)
         yield
         x = (shifted * lax.rsqrt(spread + EPSILON * x.shape[1]) * gain).astype(BF16)
         q_ref[i], k_ref[i], v_ref[i], g_ref[i] = projected(x, sides, keys, gate, scaling)
@@ -164,6 +171,7 @@
     share = length // parties
     blocks = length // LANES
     reach = LANES // share
+    half = heads // 2
     for h in range(heads):
         for t in range(blocks):
             at = (t * heads + h) * rows
@@ -196,40 +204,68 @@
         yield
         shifted = stacked - jnp.mean(stacked, axis=-1, keepdims=True)
         yield
-        spread = jnp.sum(shifted * shifted, axis=-1, keepdims=True)
+        spread = row_sums(shifted * shifted)
         yield
         x = (shifted * lax.rsqrt(spread + EPSILON * stacked.shape[1]) * gain).astype(BF16)
-        rows_ref[pl.ds(t * heads * rows + i, heads, stride=rows), :] = dot(w_tri_ref[0], x, ((1,), (1,)))
+        bias_rows = dot(w_tri_ref[0], x, ((1,), (1,)))
+        for p in range(2):
+            at = pl.ds((p * blocks + t) * half * rows + i, half, stride=rows)
+            rows_ref[at, :] = bias_rows[p * half : (p + 1) * half]
 
     in_step((stream(i, t) for i in range(rows) for t in range(blocks)), max(TOKENS // length, 1))
     packed = rows_ref[...].astype(BF16)
+    part = packed.shape[0] // 2
     for d in range(parties):
-        send_ref[d, rows * share :, :] = packed
+        send_ref[rank_out[d], rows * share :, :] = packed[d % 2 * part : (d % 2 + 1) * part]
+
+
+def hold(held_ref, got_ref, rank):
+    count = held_ref.shape[0] // len(rank)
+    for s in range(len(rank)):
+        held_ref[s * count : (s + 1) * count, :] = got_ref[rank[s], :count, :].astype(F32)
+
+
+def second_project_kernel(heads, rank, got_ref, gain_ref, w_ref, gate_bias_ref, q_ref, k_ref, v_ref, g_ref, held_ref):
+    share, length, width = k_ref.shape
+    scaling = (width // heads) ** (-0.5) * LOG2E
+    hold(held_ref, got_ref, rank)
+    sides, keys = turned_weights(w_ref[0], width)
+    gate = gate_column(gate_bias_ref[1:2, :], length)
+    gain = gain_ref[1:2, :] * held_ref.shape[1] ** 0.5
+
+    def stream(j):
+        x = held_ref[pl.ds(j, length, stride=share), :]
+        shifted = x - jnp.mean(x, axis=-1, keepdims=True)
+        yield
+        spread = row_sums(shifted * shifted)
+        yield
+        x = (shifted * lax.rsqrt(spread + EPSILON * x.shape[1]) * gain).astype(BF16)
+        q_ref[j], k_ref[j], v_ref[j], g_ref[j] = projected(x, sides, keys, gate, scaling)
+
+    in_step((stream(j) for j in range(share)), max(TOKENS // length, 1))
 
 
 def second_kernel(
-    rows, rank, got_ref, column_ref, lift_ref, gain_ref, w_ref, gate_bias_ref, w_out_ref, out_bias_ref,
+    rank, got_ref, other_ref, q_ref, k_ref, v_ref, g_ref, column_ref, lift_ref, w_out_ref, out_bias_ref,
     out_ref, held_ref, bias_ref, sems,
 ):
     parties = got_ref.shape[0]
-    length = column_ref.shape[0]
-    share = length // parties
+    share, length, width = k_ref.shape
+    rows = length // parties
     blocks = length // LANES
-    width = w_ref.shape[2] // 4
-    heads = bias_ref.shape[1] // length
-    scaling = (width // heads) ** (-0.5) * LOG2E
-    for s in range(parties):
-        held_ref[s * rows * share : (s + 1) * rows * share, :] = got_ref[rank[s], : rows * share, :].astype(F32)
-    for n in range(heads * blocks):
-        at = rows * share + n * rows
-        for s in range(parties):
-            span = slice(s * rows, (s + 1) * rows)
-            bias_ref[span, n * LANES : (n + 1) * LANES] = masked(
-                got_ref[rank[s], at : at + rows, :].astype(F32), column_ref[span, :]
-            )
-    sides, keys = turned_weights(w_ref[0], width)
-    gate = gate_column(gate_bias_ref[1:2, :], length)
-    gain = gain_ref[1:2, :] * held_ref.shape[1] ** 0.5
+    heads = bias_ref.shape[0] // blocks
+    half = heads // 2
+    hold(held_ref, got_ref, rank)
+    side = lax.rem(lax.axis_index("row"), 2)
+    for own, ref, skip in ((side, got_ref, rows * share), (1 - side, other_ref, 0)):
+        for t in range(blocks):
+            for n in range(half):
+                at = skip + (t * half + n) * rows
+                for s in range(parties):
+                    span = slice(s * rows, (s + 1) * rows)
+                    bias_ref[t * heads + own * half + n, span, :] = masked(
+                        ref[rank[s], at : at + rows, :].astype(F32), column_ref[span, :]
+                    )
 
     def piece(n):
         at = pl.ds(n * PIECE * share, PIECE * share)
@@ -240,23 +276,15 @@
     sent = [0]
 
     def stream(j):
-        x = held_ref[pl.ds(j, length, stride=share), :]
-        shifted = x - jnp.mean(x, axis=-1, keepdims=True)
-        yield
-        spread = jnp.sum(shifted * shifted, axis=-1, keepdims=True)
-        yield
-        x = (shifted * lax.rsqrt(spread + EPSILON * x.shape[1]) * gain).astype(BF16)
-        qt, k, vt, gt = projected(x, sides, keys, gate, scaling)
-        yield
         lift = lift_of(lift_ref[j : j + 1, :], length)
         for t in range(blocks):
             span = slice(t * LANES, (t + 1) * LANES)
             result = []
 
             def bias(h, t=t):
-                return bias_ref[:, (t * heads + h) * LANES : (t * heads + h + 1) * LANES]
-
-            yield from attention(k, qt[:, span], vt, gt[:, span], bias, lift, heads, result)
+                return bias_ref[t * heads + h]
+
+            yield from attention(k_ref[j], q_ref[j, :, span], v_ref[j], g_ref[j, :, span], bias, lift, heads, result)
             update = dot(result[0], w_out_ref[0], ((0,), (0,))) + out_bias_ref[1:2, :]
             yield
             for p in range(LANES // PIECE):
@@ -357,7 +385,7 @@
     send = pl.pallas_call(
         functools.partial(first_kernel, ranks(early), ranks(late)),
         grid=(1,),
-        out_shape=shape((parties, rows * share + bias_rows, LANES), BF16),
+        out_shape=shape((parties, rows * share + bias_rows // 2, LANES), BF16),
         in_specs=[full(a) for a in taken]
         + [of_pass(w_tri, 1), of_pass(w_out, 0), full(out_bias)],
         scratch_shapes=[
@@ -368,23 +396,42 @@
         name="first",
     )(*taken, w_tri, w_out, out_bias)
     got = exchange(send, late)
+    partners = [(d, d ^ 1) for d in range(parties)]
+    other = lax.ppermute(got[:, rows * share :, :], "row", partners)
+    q, k, v, g = pl.pallas_call(
+        functools.partial(second_project_kernel, heads, ranks(late)),
+        grid=(1,),
+        out_shape=(
+            shape((share, width, length), BF16),
+            shape((share, length, width), BF16),
+            shape((share, width, length), BF16),
+            shape((share, width, length), F32),
+        ),
+        in_specs=[full(got), full(ln_gain), of_pass(w_proj, 1), full(gate_bias)],
+        scratch_shapes=[pltpu.VMEM((length * share, channels), F32)],
+        compiler_params=params(),
+        cost_estimate=pl.CostEstimate(
+            flops=2 * rows * length * channels * 4 * width,
+            transcendentals=rows * length * width,
+            bytes_accessed=rows * length * width * 12,
+        ),
+        name="second_project",
+    )(got, ln_gain, w_proj, gate_bias)
+    taken = (got, other, q, k, v, g, column, lift)
     out = pl.pallas_call(
-        functools.partial(second_kernel, rows, ranks(late)),
+        functools.partial(second_kernel, ranks(late)),
         grid=(1,),
         out_shape=shape((length * share, channels), F32),
-        in_specs=[
-            full(got), full(column), full(lift), full(ln_gain), of_pass(w_proj, 1), full(gate_bias), of_pass(w_out, 1),
-            full(out_bias),
-        ],
+        in_specs=[full(a) for a in taken] + [of_pass(w_out, 1), full(out_bias)],
         out_specs=hbm,
         scratch_shapes=[
             pltpu.VMEM((length * share, channels), F32),
-            pltpu.VMEM((length, heads * length), F32),
+            pltpu.VMEM((length // LANES * heads, length, LANES), F32),
             pltpu.SemaphoreType.DMA((length // PIECE,)),
         ],
         compiler_params=params(),
         name="second",
-    )(got, column, lift, ln_gain, w_proj, gate_bias, w_out, out_bias)
+    )(*taken, w_out, out_bias)
     return out.reshape(length, share, channels)
 
 

time: 34.1 us -> 33.3 us (0.977)
  blocking collectives: 15.4 us -> 14 us
  waiting for transfers between devices: 2.27 us -> 2.97 us
    all_to_all x1, blocking collectives: 15.4 us -> 14 us  [exchange(): lax.all_to_all(parts, 'row', split_axis=0, concat_axis=0, tiled=True, axi...]
    ppermute x0 -> x1, waiting for transfers between devices: none -> 0.49 us  [local(): other = lax.ppermute(got[:, rows * share:, :], 'row', partners)]
    pallas_call x1 -> x2, Pallas kernels: 2.56 us -> 2.6 us  [the longest x1 1.85 us: local(): pl.pallas_call(functools.partial(second_kernel, ranks(late)), grid=(1,),...]
  transfers between devices with their start and end apart: 1 -> 2, of which waited for: 1 -> 2; matrix products, arithmetic and copies ran while one was open for 0% -> 0% of each run, Pallas kernels for 4% -> 6%
where the time goes in v5:
time: 33.3 us; the launch traced here: 32.9 us
  blocking collectives  14 us (42%)
  starting transfers between devices  7.58 us (23%)
  Pallas kernels  7.57 us (23%)
  waiting for transfers between devices  2.97 us (9%)
  local copies, waits for them, and re-layouts  0.65 us (2%)
    all_to_all x1, blocking collectives, exchange(): lax.all_to_all(parts, 'row', split_axis=0, concat_axis=0, tiled=True, axi...  14 us
    all_to_all x1, starting transfers between devices, exchange(): lax.all_to_all(parts, 'row', split_axis=0, concat_axis=0, tiled=True, axi...  7.57 us
    all_to_all x1, waiting for transfers between devices, exchange(): lax.all_to_all(parts, 'row', split_axis=0, concat_axis=0, tiled=True, axi...  2.48 us
    pallas_call x1, Pallas kernels, local(): pl.pallas_call(bias_kernel, grid=(1,), out_shape=shape((parties, bias_row...  2.3 us
    pallas_call x1, Pallas kernels, local(): pl.pallas_call(functools.partial(second_kernel, ranks(late)), grid=(1,),...  1.85 us
    pallas_call x1, Pallas kernels, local(): pl.pallas_call(functools.partial(first_kernel, ranks(early), ranks(late))...  1.42 us
    pallas_call x1, Pallas kernels, local(): pl.pallas_call(functools.partial(project_kernel, heads), grid=(1,), out_s...  1.25 us
    pallas_call x1, Pallas kernels, local(): pl.pallas_call(functools.partial(second_project_kernel, heads, ranks(late...  0.75 us
  transfers between devices with their start and end apart: 2, of which 2 were waited for; matrix products, arithmetic and copies ran while one was open for 0% of the time, Pallas kernels for 6%

profile of v5, /device:TPU:1, one launch (start us, length us, event | category | flops | bytes accessed | tf_op | source)
XLA Modules:
  0.0 32.9 jit_solution(10473981046735709562)
XLA Ops:
  0.0 0.0 copy-start
  0.0 0.0 copy-start.3
  0.0 0.0 copy-start.5
  0.0 0.0 copy-start.6
  0.0 2.3 %bias.1 = bf16[16,32,128]{2,1,0:T(8,128)(2,1)} custom-call(f32[8,128,128]{2,1,0:T(8,128)} %x_ref.5, f32[2,128]{1,0:T(2,128)} %gain_ref.7, bf16[2,4,128]{2,1,0:T(4,128)(2,1)} %bitcast.3), custom_call_target="tpu_custom_call" | custom-call | tf_op jit(solution)/shard_map/bias/pallas_call | solution.py:346
  2.3 0.0 copy-start.1
  2.3 7.6 %all-to-all-start = ((bf16[16,32,128]{2,1,0:T(8,128)(2,1)}), bf16[16,32,128]{2,1,0:T(8,128)(2,1)S(1)}, u32[]{:S(2)}, u32[]{:S(2)}) async-start(bf16[16,32,128]{2,1,0:T(8,128)(2,1)} %bias.1), calls=%async_computation | async-start | bytes 262144 | tf_op jit(solution)/shard_map/all_to_all | solution.py:343
  9.9 0.0 copy-start.4
  9.9 0.0 copy-start.7
  9.9 0.0 copy-done
  9.9 0.0 copy-done.3
  10.0 0.0 copy-done.5
  10.0 0.0 copy-done.6
  10.0 0.0 copy-done.1
  10.0 0.6 %copy-done.4 = f32[2,128]{1,0:T(2,128)S(1)} copy-done((f32[2,128]{1,0:T(2,128)S(1)}, f32[2,128]{1,0:T(2,128)}, u32[]{:S(2)}) %copy-start.4) | copy-done | bytes 1048
  10.6 0.0 copy-done.7
  10.6 0.0 copy-start.2
  10.6 1.3 %project.1 = (bf16[8,128,128]{2,1,0:T(8,128)(2,1)S(1)}, bf16[8,128,128]{2,1,0:T(8,128)(2,1)S(1)}, bf16[8,128,128]{2,1,0:T(8,128)(2,1)S(1)}, f32[8,128,128]{2,1,0...) custom-call(f32[8,128,128]{2,1,0:T(8,128)S(1)} %copy-done, f32[2,128]{1,0:T(2,128)S(1)} %copy-done.4, ...), custom_call_target="tpu_custom_call" | custom-call | flops 134217728 | bytes 1572864 | tf_op jit(solution)/shard_map/project/pallas_call | solution.py:363
  11.9 2.5 %all-to-all-done.got_ref = bf16[16,32,128]{2,1,0:T(8,128)(2,1)S(1)} async-done(((bf16[16,32,128]{2,1,0:T(8,128)(2,1)}), bf16[16,32,128]{2,1,0:T(8,128)(2,1)S(1)}, u32[]{:S(2)}, u32[]{:S(2)}) %all-to-all-start) | async-done | bytes 131104 | tf_op jit(solution)/shard_map/all_to_all | solution.py:343
  14.3 0.0 copy-done.2
  14.3 1.4 %first.1 = bf16[16,80,128]{2,1,0:T(8,128)(2,1)S(1)} custom-call(f32[8,128,128]{2,1,0:T(8,128)S(1)} %copy-done, bf16[8,128,128]{2,1,0:T(8,128)(2,1)S(1)} %get-tuple-element.15.q_ref, bf16[8,128,128]{2,1,0:T(8,128)(2,1)S(1)} %get-tuple-element.16.k_ref, bf16[8,128,128]{2,1,0:T(8,128)(2,1)S(1)} %get-tuple-element.17.v_ref, ...), custom_call_target="tpu_custom_call" | custom-call | tf_op jit(solution)/shard_map/first/pallas_call | solution.py:385
  15.8 14.0 %all_to_all.10.got_ref = bf16[16,80,128]{2,1,0:T(8,128)(2,1)S(1)} all-to-all(bf16[16,80,128]{2,1,0:T(8,128)(2,1)S(1)} %first.1), channel_id=1, replica_groups={{9,8,4,12,0,5,13,1,10,6,14,2,11,7,15,3},{25,24,20,28,16,21,29,17,26,22,..., dimensions={0} | all-to-all | bytes 655360 | tf_op jit(solution)/shard_map/all_to_all | solution.py:343
  29.8 0.0 collective-permute-start
  29.8 0.7 %second_project.1 = (bf16[8,128,128]{2,1,0:T(8,128)(2,1)S(1)}, bf16[8,128,128]{2,1,0:T(8,128)(2,1)S(1)}, bf16[8,128,128]{2,1,0:T(8,128)(2,1)S(1)}, f32[8,128,128]{2,1,0:T(8,128)S(1)}) custom-call(bf16[16,80,128]{2,1,0:T(8,128)(2,1)S(1)} %all_to_all.10.got_ref, f32[2,128]{1,0:T(2,128)S(1)} %copy-done.4, bf16[2,128,512]{2,1,0:T(8,128)(2,1)S(1)} %copy-done.1, ...), custom_call_target="tpu_custom_call" | custom-call | flops 134217728 | bytes 1572864 | tf_op jit(solution)/shard_map/second_project/pallas_call | solution.py:401
  30.6 0.5 %collective-permute-done.other_ref = bf16[16,16,128]{2,1,0:T(8,128)(2,1)S(1)} collective-permute-done((bf16[16,16,128]{2,1,0:T(8,128)(2,1)S(1)}, bf16[16,16,128]{2,1,0:T(8,128)(2,1)S(1)}, u32[]{:S(2)}, u32[]{:S(2)}) %collective-permute-start) | collective-permute-done | bytes 65568 | tf_op jit(solution)/shard_map/ppermute | solution.py:400
  31.1 1.9 %second.1 = f32[1024,128]{1,0:T(8,128)} custom-call(bf16[16,80,128]{2,1,0:T(8,128)(2,1)S(1)} %all_to_all.10.got_ref, bf16[16,16,128]{2,1,0:T(8,128)(2,1)S(1)} %collective-permute-done.other_ref, bf16[8,128,128]{2,1,0:T(8,128)(2,1)S(1)} %get-tuple-element.21.q_ref, bf16[8,128,128]{2,1,0:T(8,128)(2,1)S(1)} %get-tuple-element.22.k_ref, ...), custom_call_target="tpu_custom_call" | custom-call | tf_op jit(solution)/shard_map/second/pallas_call | solution.py:421
  (1 shorter events, 0.0 us)
Async XLA Ops:
  0.0 9.9 %copy-start = (f32[8,128,128]{2,1,0:T(8,128)S(1)}, f32[8,128,128]{2,1,0:T(8,128)}, u32[]{:S(2)}) copy-start(f32[8,128,128]{2,1,0:T(8,128)} %x_ref.5) | copy-start | bytes 1572868
  0.0 9.9 %copy-start.3 = (bf16[2,128,4]{1,2,0:T(4,128)(2,1)S(1)}, bf16[2,128,4]{1,2,0:T(4,128)(2,1)}, u32[]{:S(2)}) copy-start(bf16[2,128,4]{1,2,0:T(4,128)(2,1)} %param.12) | copy-start | bytes 6148
  0.0 10.0 %copy-start.5 = (f32[2,128]{1,0:T(2,128)S(1)}, f32[2,128]{1,0:T(2,128)}, u32[]{:S(2)}) copy-start(f32[2,128]{1,0:T(2,128)} %out_bias_ref.3) | copy-start | bytes 3076
  0.0 10.0 %copy-start.6 = (f32[2,128]{1,0:T(2,128)S(1)}, f32[2,128]{1,0:T(2,128)}, u32[]{:S(2)}) copy-start(f32[2,128]{1,0:T(2,128)} %gate_bias_ref.3) | copy-start | bytes 3076
  2.3 7.6 %copy-start.1 = (bf16[2,128,512]{2,1,0:T(8,128)(2,1)S(1)}, bf16[2,128,512]{2,1,0:T(8,128)(2,1)}, u32[]{:S(2)}) copy-start(bf16[2,128,512]{2,1,0:T(8,128)(2,1)} %w_ref.3) | copy-start | bytes 786436
  2.3 12.0 %all-to-all-start = ((bf16[16,32,128]{2,1,0:T(8,128)(2,1)}), bf16[16,32,128]{2,1,0:T(8,128)(2,1)S(1)}, u32[]{:S(2)}, u32[]{:S(2)}) async-start(bf16[16,32,128]{2,1,0:T(8,128)(2,1)} %bias.1), calls=%async_computation | async-start | bytes 262144 | tf_op jit(solution)/shard_map/all_to_all | solution.py:343
  9.9 0.7 %copy-start.4 = (f32[2,128]{1,0:T(2,128)S(1)}, f32[2,128]{1,0:T(2,128)}, u32[]{:S(2)}) copy-start(f32[2,128]{1,0:T(2,128)} %gain_ref.7) | copy-start | bytes 3076
  9.9 0.7 %copy-start.7 = (s32[128]{0:T(128)S(1)}, s32[128]{0:T(128)}, u32[]{:S(2)}) copy-start(s32[128]{0:T(128)} %flag_ref.1) | copy-start | bytes 1540
  10.6 3.7 %copy-start.2 = (bf16[2,128,128]{2,1,0:T(8,128)(2,1)S(1)}, bf16[2,128,128]{2,1,0:T(8,128)(2,1)}, u32[]{:S(2)}) copy-start(bf16[2,128,128]{2,1,0:T(8,128)(2,1)} %w_out_ref.3) | copy-start | bytes 196612
  29.8 1.3 %collective-permute-start = (bf16[16,16,128]{2,1,0:T(8,128)(2,1)S(1)}, bf16[16,16,128]{2,1,0:T(8,128)(2,1)S(1)}, u32[]{:S(2)}, u32[]{:S(2)}) collective-permute-start(bf16[16,16,128]{2,1,0:T(8,128)(2,1)S(1)} %slice.4), channel_id=1, source_target_pairs={{0,1},{1,0},{2,3},{3,2},{4,5},{5,4},{6,7},{7,6},{8,9},{9,8},{10,11... | collective-permute-start | bytes 196616 | tf_op jit(solution)/shard_map/ppermute | solution.py:400

commit v6 on v5

--- a/solution.py
+++ b/solution.py
@@ -10,7 +10,7 @@
 LANES = 128
 VMEM_BYTES = 24 * 2**20
 KEPT = 2
-PIECE = 32
+PIECE = 64
 TOKENS = 1024
 F32 = jnp.float32
 BF16 = jnp.bfloat16
@@ -246,7 +246,7 @@
 
 
 def second_kernel(
-    rank, got_ref, other_ref, q_ref, k_ref, v_ref, g_ref, column_ref, lift_ref, w_out_ref, out_bias_ref,
+    rank, got_ref, other_ref, stacked_ref, q_ref, k_ref, v_ref, g_ref, column_ref, lift_ref, w_out_ref, out_bias_ref,
     out_ref, held_ref, bias_ref, sems,
 ):
     parties = got_ref.shape[0]
@@ -255,7 +255,6 @@
     blocks = length // LANES
     heads = bias_ref.shape[0] // blocks
     half = heads // 2
-    hold(held_ref, got_ref, rank)
     side = lax.rem(lax.axis_index("row"), 2)
     for own, ref, skip in ((side, got_ref, rows * share), (1 - side, other_ref, 0)):
         for t in range(blocks):
@@ -289,7 +288,7 @@
             yield
             for p in range(LANES // PIECE):
                 at = pl.ds((t * LANES + p * PIECE) * share + j, PIECE, stride=share)
-                held_ref[at, :] = held_ref[at, :] + update[p * PIECE : (p + 1) * PIECE]
+                held_ref[at, :] = stacked_ref[at, :] + update[p * PIECE : (p + 1) * PIECE]
                 stored[t * (LANES // PIECE) + p] += 1
                 while sent[0] < len(copies) and stored[min(sent[0] + 1, len(copies) - 1)] == share:
                     copies[sent[0]].start()
@@ -398,7 +397,7 @@
     got = exchange(send, late)
     partners = [(d, d ^ 1) for d in range(parties)]
     other = lax.ppermute(got[:, rows * share :, :], "row", partners)
-    q, k, v, g = pl.pallas_call(
+    q, k, v, g, stacked = pl.pallas_call(
         functools.partial(second_project_kernel, heads, ranks(late)),
         grid=(1,),
         out_shape=(
@@ -406,9 +405,9 @@
             shape((share, length, width), BF16),
             shape((share, width, length), BF16),
             shape((share, width, length), F32),
+            shape((length * share, channels), F32),
         ),
         in_specs=[full(got), full(ln_gain), of_pass(w_proj, 1), full(gate_bias)],
-        scratch_shapes=[pltpu.VMEM((length * share, channels), F32)],
         compiler_params=params(),
         cost_estimate=pl.CostEstimate(
             flops=2 * rows * length * channels * 4 * width,
@@ -417,7 +416,7 @@
         ),
         name="second_project",
     )(got, ln_gain, w_proj, gate_bias)
-    taken = (got, other, q, k, v, g, column, lift)
+    taken = (got, other, stacked, q, k, v, g, column, lift)
     out = pl.pallas_call(
         functools.partial(second_kernel, ranks(late)),
         grid=(1,),

time: 33.3 us -> 33.3 us (level)
  no operation moved by 1% of the time
where the time goes in v6:
time: 33.3 us; the launch traced here: 32.9 us
  blocking collectives  14 us (42%)
  starting transfers between devices  7.58 us (23%)
  Pallas kernels  7.55 us (23%)
  waiting for transfers between devices  2.97 us (9%)
  local copies, waits for them, and re-layouts  0.65 us (2%)
    all_to_all x1, blocking collectives, exchange(): lax.all_to_all(parts, 'row', split_axis=0, concat_axis=0, tiled=True, axi...  14 us
    all_to_all x1, starting transfers between devices, exchange(): lax.all_to_all(parts, 'row', split_axis=0, concat_axis=0, tiled=True, axi...  7.57 us
    all_to_all x1, waiting for transfers between devices, exchange(): lax.all_to_all(parts, 'row', split_axis=0, concat_axis=0, tiled=True, axi...  2.48 us
    pallas_call x1, Pallas kernels, local(): pl.pallas_call(bias_kernel, grid=(1,), out_shape=shape((parties, bias_row...  2.3 us
    pallas_call x1, Pallas kernels, local(): pl.pallas_call(functools.partial(second_kernel, ranks(late)), grid=(1,),...  1.83 us
    pallas_call x1, Pallas kernels, local(): pl.pallas_call(functools.partial(first_kernel, ranks(early), ranks(late))...  1.42 us
    pallas_call x1, Pallas kernels, local(): pl.pallas_call(functools.partial(project_kernel, heads), grid=(1,), out_s...  1.25 us
    pallas_call x1, Pallas kernels, local(): pl.pallas_call(functools.partial(second_project_kernel, heads, ranks(late...  0.75 us
  transfers between devices with their start and end apart: 2, of which 2 were waited for; matrix products, arithmetic and copies ran while one was open for 0% of the time, Pallas kernels for 6%

profile of v6, /device:TPU:1, one launch (start us, length us, event | category | flops | bytes accessed | tf_op | source)
XLA Modules:
  0.0 32.9 jit_solution(10555622456989976148)
XLA Ops:
  0.0 0.0 copy-start
  0.0 0.0 copy-start.3
  0.0 0.0 copy-start.5
  0.0 0.0 copy-start.6
  0.0 2.3 %bias.1 = bf16[16,32,128]{2,1,0:T(8,128)(2,1)} custom-call(f32[8,128,128]{2,1,0:T(8,128)} %x_ref.5, f32[2,128]{1,0:T(2,128)} %gain_ref.7, bf16[2,4,128]{2,1,0:T(4,128)(2,1)} %bitcast.3), custom_call_target="tpu_custom_call" | custom-call | tf_op jit(solution)/shard_map/bias/pallas_call | solution.py:345
  2.3 0.0 copy-start.1
  2.3 7.6 %all-to-all-start = ((bf16[16,32,128]{2,1,0:T(8,128)(2,1)}), bf16[16,32,128]{2,1,0:T(8,128)(2,1)S(1)}, u32[]{:S(2)}, u32[]{:S(2)}) async-start(bf16[16,32,128]{2,1,0:T(8,128)(2,1)} %bias.1), calls=%async_computation | async-start | bytes 262144 | tf_op jit(solution)/shard_map/all_to_all | solution.py:342
  9.9 0.0 copy-start.4
  9.9 0.0 copy-start.7
  9.9 0.0 copy-done
  9.9 0.0 copy-done.3
  10.0 0.0 copy-done.5
  10.0 0.0 copy-done.6
  10.0 0.0 copy-done.1
  10.0 0.6 %copy-done.4 = f32[2,128]{1,0:T(2,128)S(1)} copy-done((f32[2,128]{1,0:T(2,128)S(1)}, f32[2,128]{1,0:T(2,128)}, u32[]{:S(2)}) %copy-start.4) | copy-done | bytes 1048
  10.6 0.0 copy-done.7
  10.6 0.0 copy-start.2
  10.6 1.3 %project.1 = (bf16[8,128,128]{2,1,0:T(8,128)(2,1)S(1)}, bf16[8,128,128]{2,1,0:T(8,128)(2,1)S(1)}, bf16[8,128,128]{2,1,0:T(8,128)(2,1)S(1)}, f32[8,128,128]{2,1,0...) custom-call(f32[8,128,128]{2,1,0:T(8,128)S(1)} %copy-done, f32[2,128]{1,0:T(2,128)S(1)} %copy-done.4, ...), custom_call_target="tpu_custom_call" | custom-call | flops 134217728 | bytes 1572864 | tf_op jit(solution)/shard_map/project/pallas_call | solution.py:362
  11.9 2.5 %all-to-all-done.got_ref = bf16[16,32,128]{2,1,0:T(8,128)(2,1)S(1)} async-done(((bf16[16,32,128]{2,1,0:T(8,128)(2,1)}), bf16[16,32,128]{2,1,0:T(8,128)(2,1)S(1)}, u32[]{:S(2)}, u32[]{:S(2)}) %all-to-all-start) | async-done | bytes 131104 | tf_op jit(solution)/shard_map/all_to_all | solution.py:342
  14.3 0.0 copy-done.2
  14.3 1.4 %first.1 = bf16[16,80,128]{2,1,0:T(8,128)(2,1)S(1)} custom-call(f32[8,128,128]{2,1,0:T(8,128)S(1)} %copy-done, bf16[8,128,128]{2,1,0:T(8,128)(2,1)S(1)} %get-tuple-element.16.q_ref, bf16[8,128,128]{2,1,0:T(8,128)(2,1)S(1)} %get-tuple-element.17.k_ref, bf16[8,128,128]{2,1,0:T(8,128)(2,1)S(1)} %get-tuple-element.18.v_ref, ...), custom_call_target="tpu_custom_call" | custom-call | tf_op jit(solution)/shard_map/first/pallas_call | solution.py:384
  15.8 14.0 %all_to_all.10.got_ref = bf16[16,80,128]{2,1,0:T(8,128)(2,1)S(1)} all-to-all(bf16[16,80,128]{2,1,0:T(8,128)(2,1)S(1)} %first.1), channel_id=1, replica_groups={{9,8,4,12,0,5,13,1,10,6,14,2,11,7,15,3},{25,24,20,28,16,21,29,17,26,22,..., dimensions={0} | all-to-all | bytes 655360 | tf_op jit(solution)/shard_map/all_to_all | solution.py:342
  29.8 0.0 collective-permute-start
  29.8 0.7 %second_project.1 = (bf16[8,128,128]{2,1,0:T(8,128)(2,1)S(1)}, bf16[8,128,128]{2,1,0:T(8,128)(2,1)S(1)}, bf16[8,128,128]{2,1,0:T(8,128)(2,1)S(1)}, f32[8,128,128]{2,1,0:T(8,128)S(1)}, f32[1024,128]{1,0:T(8,128)S(1)}) custom-call(bf16[16,80,128]{2,1,0:T(8,128)(2,1)S(1)} %all_to_all.10.got_ref, f32[2,128]{1,0:T(2,128)S(1)} %copy-done.4, ...), custom_call_target="tpu_custom_call" | custom-call | flops 134217728 | bytes 1572864 | tf_op jit(solution)/shard_map/second_project/pallas_call | solution.py:400
  30.6 0.5 %collective-permute-done.other_ref = bf16[16,16,128]{2,1,0:T(8,128)(2,1)S(1)} collective-permute-done((bf16[16,16,128]{2,1,0:T(8,128)(2,1)S(1)}, bf16[16,16,128]{2,1,0:T(8,128)(2,1)S(1)}, u32[]{:S(2)}, u32[]{:S(2)}) %collective-permute-start) | collective-permute-done | bytes 65568 | tf_op jit(solution)/shard_map/ppermute | solution.py:399
  31.1 1.8 %second.1 = f32[1024,128]{1,0:T(8,128)} custom-call(bf16[16,80,128]{2,1,0:T(8,128)(2,1)S(1)} %all_to_all.10.got_ref, bf16[16,16,128]{2,1,0:T(8,128)(2,1)S(1)} %collective-permute-done.other_ref, f32[1024,128]{1,0:T(8,128)S(1)} %get-tuple-element.22.stacked_ref, bf16[8,128,128]{2,1,0:T(8,128)(2,1)S(1)} %get-tuple-element.23.q_ref, ...), custom_call_target="tpu_custom_call" | custom-call | tf_op jit(solution)/shard_map/second/pallas_call | solution.py:420
  (1 shorter events, 0.0 us)
Async XLA Ops:
  0.0 9.9 %copy-start = (f32[8,128,128]{2,1,0:T(8,128)S(1)}, f32[8,128,128]{2,1,0:T(8,128)}, u32[]{:S(2)}) copy-start(f32[8,128,128]{2,1,0:T(8,128)} %x_ref.5) | copy-start | bytes 1572868
  0.0 9.9 %copy-start.3 = (bf16[2,128,4]{1,2,0:T(4,128)(2,1)S(1)}, bf16[2,128,4]{1,2,0:T(4,128)(2,1)}, u32[]{:S(2)}) copy-start(bf16[2,128,4]{1,2,0:T(4,128)(2,1)} %param.12) | copy-start | bytes 6148
  0.0 10.0 %copy-start.5 = (f32[2,128]{1,0:T(2,128)S(1)}, f32[2,128]{1,0:T(2,128)}, u32[]{:S(2)}) copy-start(f32[2,128]{1,0:T(2,128)} %out_bias_ref.3) | copy-start | bytes 3076
  0.0 10.0 %copy-start.6 = (f32[2,128]{1,0:T(2,128)S(1)}, f32[2,128]{1,0:T(2,128)}, u32[]{:S(2)}) copy-start(f32[2,128]{1,0:T(2,128)} %gate_bias_ref.3) | copy-start | bytes 3076
  2.3 7.6 %copy-start.1 = (bf16[2,128,512]{2,1,0:T(8,128)(2,1)S(1)}, bf16[2,128,512]{2,1,0:T(8,128)(2,1)}, u32[]{:S(2)}) copy-start(bf16[2,128,512]{2,1,0:T(8,128)(2,1)} %w_ref.3) | copy-start | bytes 786436
  2.3 12.0 %all-to-all-start = ((bf16[16,32,128]{2,1,0:T(8,128)(2,1)}), bf16[16,32,128]{2,1,0:T(8,128)(2,1)S(1)}, u32[]{:S(2)}, u32[]{:S(2)}) async-start(bf16[16,32,128]{2,1,0:T(8,128)(2,1)} %bias.1), calls=%async_computation | async-start | bytes 262144 | tf_op jit(solution)/shard_map/all_to_all | solution.py:342
  9.9 0.7 %copy-start.4 = (f32[2,128]{1,0:T(2,128)S(1)}, f32[2,128]{1,0:T(2,128)}, u32[]{:S(2)}) copy-start(f32[2,128]{1,0:T(2,128)} %gain_ref.7) | copy-start | bytes 3076
  9.9 0.7 %copy-start.7 = (s32[128]{0:T(128)S(1)}, s32[128]{0:T(128)}, u32[]{:S(2)}) copy-start(s32[128]{0:T(128)} %flag_ref.1) | copy-start | bytes 1540
  10.6 3.7 %copy-start.2 = (bf16[2,128,128]{2,1,0:T(8,128)(2,1)S(1)}, bf16[2,128,128]{2,1,0:T(8,128)(2,1)}, u32[]{:S(2)}) copy-start(bf16[2,128,128]{2,1,0:T(8,128)(2,1)} %w_out_ref.3) | copy-start | bytes 196612
  29.8 1.3 %collective-permute-start = (bf16[16,16,128]{2,1,0:T(8,128)(2,1)S(1)}, bf16[16,16,128]{2,1,0:T(8,128)(2,1)S(1)}, u32[]{:S(2)}, u32[]{:S(2)}) collective-permute-start(bf16[16,16,128]{2,1,0:T(8,128)(2,1)S(1)} %slice.4), channel_id=1, source_target_pairs={{0,1},{1,0},{2,3},{3,2},{4,5},{5,4},{6,7},{7,6},{8,9},{9,8},{10,11... | collective-permute-start | bytes 196616 | tf_op jit(solution)/shard_map/ppermute | solution.py:399
